TPU v7x, 256 devices: a whole 4x4x8 slice. The times are simulated.
256 devices in a mesh: section: 2 (over core), seq: 16 (over y, x), traj: 8 (over z).
Axes of the slice: x: 4, y: 4, z: 8, core: 2. Of those that a mesh axis runs over, the one named last changes fastest.
Arguments:
- tokens: bfloat16 [16384, 2048], P(('traj', 'seq')), parts along dimension 0, may hold values from -6 to 6
- norm_gain: float32 [2, 2048], P('section'), may hold values from 0.25 to 1.75
- w_qkv: bfloat16 [2, 2048, 3072], P('section'), may hold values from -0.125 to 0.125
- w_rate: bfloat16 [2, 2048, 16], P('section'), may hold values from -0.125 to 0.125
- rate_base: float32 [2, 16], P('section'), may hold values from 0.00625 to 0.015625
- init_state: float32 [2, 16, 64, 64], P('section'), may hold values from -6 to 6
- w_out: bfloat16 [2, 1024, 2048], P('section'), may hold values from -0.1875 to 0.1875
Outputs:
- layer_out: bfloat16 [2, 16384, 2048], P('section', ('traj', 'seq')), parts along dimension 1
There are 8 independent parts, one for each index of `traj`. A program takes and returns all parts, laid end to end along the dimension named above; an argument that names none is the same for every part. Nothing has to cross between parts.
All inputs are finite; a program needn't handle non-finite values.
Results may differ from a plain program's by a relative error of at most 0.017.
Values may be sent and summed in bfloat16 or wider, within the bound.
A program may use at most 128 MiB of HBM per device.

v0:
```python
import jax
import jax.numpy as jnp
from jax import lax
from jax.sharding import PartitionSpec as P

HD = 64
MB = 64


def from_behind(value, axis, steps):
    count = lax.axis_size(axis)
    initial, last = (max(0, -steps), min(count, count - steps))
    return lax.ppermute(value, axis, [(source, source + steps) for source in range(initial, last)])


def inner_block(weight_state, block):
    precise_mode = lax.Precision.HIGHEST
    query_rows, key_input, value_input, rates = block
    predicted_values = jnp.einsum("ylc,yci->yli", key_input, weight_state, precision=precise_mode)
    scaled_gradient = rates[..., None] * (predicted_values - value_input)
    causal_mask = jnp.tril(jnp.ones((query_rows.shape[1], query_rows.shape[1]), query_rows.dtype))
    attention_scores = (
        jnp.einsum("kxw,kqw->kxq", query_rows, key_input, precision=precise_mode) * causal_mask
    )
    inner_output = jnp.einsum(
        "ylc,yci->yli", query_rows, weight_state, precision=precise_mode
    ) - jnp.einsum("ixb,ibt->ixt", attention_scores, scaled_gradient, precision=precise_mode)
    updated_state = weight_state - jnp.einsum(
        "ncz,ncp->nzp", key_input, scaled_gradient, precision=precise_mode
    )
    return (updated_state, inner_output)


def inner_inputs(hidden, gain, w_qkv, w_rate, rate_base):
    wide = hidden.astype(jnp.float32)
    mean_sq = jnp.mean(wide * wide, axis=-1, keepdims=True)
    normed = (wide * lax.rsqrt(mean_sq + 1e-06) * gain).astype(jnp.bfloat16)
    projected = jnp.dot(normed, w_qkv, preferred_element_type=jnp.float32)
    rows = hidden.shape[0]
    heads = rate_base.shape[0]
    width = heads * HD
    query_rows = projected[:, :width].reshape(rows, heads, HD)
    key_input = projected[:, width : 2 * width].reshape(rows, heads, HD)
    value_input = projected[:, 2 * width :].reshape(rows, heads, HD)
    query_rows = query_rows * lax.rsqrt(
        jnp.sum(query_rows * query_rows, axis=-1, keepdims=True) + 1e-06
    )
    key_input = key_input * lax.rsqrt(
        jnp.sum(key_input * key_input, axis=-1, keepdims=True) + 1e-06
    )
    rates = rate_base[None, :] * jax.nn.sigmoid(
        jnp.dot(normed, w_rate, preferred_element_type=jnp.float32)
    )
    blocks = rows // MB

    def to_blocks(array):
        return array.reshape(blocks, MB, heads, HD).transpose(0, 2, 1, 3)

    rate_blocks = rates.reshape(blocks, MB, heads).transpose(0, 2, 1)
    return (to_blocks(query_rows), to_blocks(key_input), to_blocks(value_input), rate_blocks)


def apply_map(linear_output, position_offset, weight_state):
    return (
        jnp.einsum("hde,hef->hdf", linear_output, weight_state, precision=lax.Precision.HIGHEST)
        + position_offset
    )


def compose_maps(earlier, later):
    return (
        jnp.einsum("hde,hef->hdf", later[0], earlier[0], precision=lax.Precision.HIGHEST),
        apply_map(later[0], later[1], earlier[1]),
    )


def block_map(carry, block):
    precise_mode = lax.Precision.HIGHEST
    query_rows, key_input, value_input, rates = block
    weighted_values = rates[..., None] * key_input
    identity_matrix = jnp.broadcast_to(
        jnp.eye(key_input.shape[2], dtype=jnp.float32), carry[0].shape
    )
    linear_output = identity_matrix - jnp.einsum(
        "ncz,ncp->nzp", key_input, weighted_values, precision=precise_mode
    )
    position_offset = jnp.einsum(
        "ncz,ncp->nzp", weighted_values, value_input, precision=precise_mode
    )
    return (compose_maps(carry, (linear_output, position_offset)), None)


def layer_terms(hidden, gain, w_qkv, w_rate, rate_base, init_state, w_out):
    blocks = inner_inputs(hidden, gain, w_qkv, w_rate, rate_base)
    identity_matrix = jnp.broadcast_to(
        jnp.eye(init_state.shape[1], dtype=jnp.float32), init_state.shape
    )
    empty = jnp.zeros_like(init_state)
    slab_map, unused = lax.scan(block_map, (identity_matrix, empty), blocks)
    seq_index = lax.axis_index("seq")

    def relay(turn_index, start_state):
        slab_end = apply_map(slab_map[0], slab_map[1], start_state)
        received = from_behind(slab_end, "seq", 1)
        return jnp.where(seq_index == 0, init_state, received)

    start_state = lax.fori_loop(0, lax.axis_size("seq") - 1, relay, init_state)
    final_state, inner_output = lax.scan(inner_block, start_state, blocks)
    rows = hidden.shape[0]
    inner_bf = inner_output.transpose(0, 2, 1, 3).reshape(rows, -1).astype(jnp.bfloat16)
    return jnp.dot(inner_bf, w_out, preferred_element_type=jnp.float32)


def shards(tokens, norm_gain, w_qkv, w_rate, rate_base, init_state, w_out):
    count = lax.axis_size("section")
    section_index = lax.axis_index("section")
    kept = jnp.zeros_like(tokens)
    current = tokens
    for round_index in range(count):
        mixed = layer_terms(
            current, norm_gain[0], w_qkv[0], w_rate[0], rate_base[0], init_state[0], w_out[0]
        )
        result = (current.astype(jnp.float32) + mixed).astype(jnp.bfloat16)
        kept = jnp.where(section_index == round_index, result, kept)
        if round_index + 1 < count:
            current = from_behind(result, "section", 1)
    return kept[None]


def solution(mesh):
    return jax.shard_map(
        shards,
        mesh=mesh,
        in_specs=(
            P(("traj", "seq"), None),
            P("section", None),
            P("section", None, None),
            P("section", None, None),
            P("section", None),
            P("section", None, None, None),
            P("section", None, None),
        ),
        out_specs=P("section", ("traj", "seq"), None),
        check_vma=False,
    )
```

profile of v0, /device:TPU:8, one launch (start us, length us, event | category | flops | bytes accessed | tf_op | source)
XLA Modules:
  0.0 644.0 jit_solution(1212496764782931938)
XLA Ops:
  26.6 276.6 %while.74 = (s32[]{:T(128)}, f32[16,64,64]{2,1,0:T(8,128)S(1)}, pred[]{:T(512)}, f32[16,64,64]{2,1,0:T(8,128)S(1)}, f32[16,64,64]{2,1,0:T(8,128)S(1)}, /*index=5*/f32[16,64,64]{2,1,0:T(8,128)S(1)}, s32[]{:T(128)}) while((s32[]{:T(128)}, f32[16,64,64]{2,1,0:T(8,128)S(1)}, pred[]{:T(512)}, f32[16,64,64]{2,1,0:T(8,128)S(1)}, ...), condition=%wide.region_5.6_spmd, body=%wide.region_4.5_spmd.sunk | while | flops 50462720 | bytes 3932306 | solution.py:107
  31.4 14.5 %collective-permute-done = f32[16,64,64]{2,1,0:T(8,128)S(1)} collective-permute-done((f32[16,64,64]{2,1,0:T(8,128)}, f32[16,64,64]{2,1,0:T(8,128)S(1)}, u32[]{:S(2)}, u32[]{:S(2)}) %collective-permute-start) | collective-permute-done | bytes 262176 | tf_op jit(solution)/shard_map/while/body/eval_jaxpr/ppermute | solution.py:13
  51.2 15.1 %collective-permute-done = f32[16,64,64]{2,1,0:T(8,128)S(1)} collective-permute-done((f32[16,64,64]{2,1,0:T(8,128)}, f32[16,64,64]{2,1,0:T(8,128)S(1)}, u32[]{:S(2)}, u32[]{:S(2)}) %collective-permute-start) | collective-permute-done | bytes 262176 | tf_op jit(solution)/shard_map/while/body/eval_jaxpr/ppermute | solution.py:13
  71.5 14.2 %collective-permute-done = f32[16,64,64]{2,1,0:T(8,128)S(1)} collective-permute-done((f32[16,64,64]{2,1,0:T(8,128)}, f32[16,64,64]{2,1,0:T(8,128)S(1)}, u32[]{:S(2)}, u32[]{:S(2)}) %collective-permute-start) | collective-permute-done | bytes 262176 | tf_op jit(solution)/shard_map/while/body/eval_jaxpr/ppermute | solution.py:13
  91.0 13.2 %collective-permute-done = f32[16,64,64]{2,1,0:T(8,128)S(1)} collective-permute-done((f32[16,64,64]{2,1,0:T(8,128)}, f32[16,64,64]{2,1,0:T(8,128)S(1)}, u32[]{:S(2)}, u32[]{:S(2)}) %collective-permute-start) | collective-permute-done | bytes 262176 | tf_op jit(solution)/shard_map/while/body/eval_jaxpr/ppermute | solution.py:13
  109.5 12.3 %collective-permute-done = f32[16,64,64]{2,1,0:T(8,128)S(1)} collective-permute-done((f32[16,64,64]{2,1,0:T(8,128)}, f32[16,64,64]{2,1,0:T(8,128)S(1)}, u32[]{:S(2)}, u32[]{:S(2)}) %collective-permute-start) | collective-permute-done | bytes 262176 | tf_op jit(solution)/shard_map/while/body/eval_jaxpr/ppermute | solution.py:13
  127.0 11.5 %collective-permute-done = f32[16,64,64]{2,1,0:T(8,128)S(1)} collective-permute-done((f32[16,64,64]{2,1,0:T(8,128)}, f32[16,64,64]{2,1,0:T(8,128)S(1)}, u32[]{:S(2)}, u32[]{:S(2)}) %collective-permute-start) | collective-permute-done | bytes 262176 | tf_op jit(solution)/shard_map/while/body/eval_jaxpr/ppermute | solution.py:13
  177.2 11.5 %collective-permute-done = f32[16,64,64]{2,1,0:T(8,128)S(1)} collective-permute-done((f32[16,64,64]{2,1,0:T(8,128)}, f32[16,64,64]{2,1,0:T(8,128)S(1)}, u32[]{:S(2)}, u32[]{:S(2)}) %collective-permute-start) | collective-permute-done | bytes 262176 | tf_op jit(solution)/shard_map/while/body/eval_jaxpr/ppermute | solution.py:13
  194.0 11.7 %collective-permute-done = f32[16,64,64]{2,1,0:T(8,128)S(1)} collective-permute-done((f32[16,64,64]{2,1,0:T(8,128)}, f32[16,64,64]{2,1,0:T(8,128)S(1)}, u32[]{:S(2)}, u32[]{:S(2)}) %collective-permute-start) | collective-permute-done | bytes 262176 | tf_op jit(solution)/shard_map/while/body/eval_jaxpr/ppermute | solution.py:13
  211.0 12.8 %collective-permute-done = f32[16,64,64]{2,1,0:T(8,128)S(1)} collective-permute-done((f32[16,64,64]{2,1,0:T(8,128)}, f32[16,64,64]{2,1,0:T(8,128)S(1)}, u32[]{:S(2)}, u32[]{:S(2)}) %collective-permute-start) | collective-permute-done | bytes 262176 | tf_op jit(solution)/shard_map/while/body/eval_jaxpr/ppermute | solution.py:13
  229.0 13.9 %collective-permute-done = f32[16,64,64]{2,1,0:T(8,128)S(1)} collective-permute-done((f32[16,64,64]{2,1,0:T(8,128)}, f32[16,64,64]{2,1,0:T(8,128)S(1)}, u32[]{:S(2)}, u32[]{:S(2)}) %collective-permute-start) | collective-permute-done | bytes 262176 | tf_op jit(solution)/shard_map/while/body/eval_jaxpr/ppermute | solution.py:13
  248.2 15.0 %collective-permute-done = f32[16,64,64]{2,1,0:T(8,128)S(1)} collective-permute-done((f32[16,64,64]{2,1,0:T(8,128)}, f32[16,64,64]{2,1,0:T(8,128)S(1)}, u32[]{:S(2)}, u32[]{:S(2)}) %collective-permute-start) | collective-permute-done | bytes 262176 | tf_op jit(solution)/shard_map/while/body/eval_jaxpr/ppermute | solution.py:13
  268.4 16.1 %collective-permute-done = f32[16,64,64]{2,1,0:T(8,128)S(1)} collective-permute-done((f32[16,64,64]{2,1,0:T(8,128)}, f32[16,64,64]{2,1,0:T(8,128)S(1)}, u32[]{:S(2)}, u32[]{:S(2)}) %collective-permute-start) | collective-permute-done | bytes 262176 | tf_op jit(solution)/shard_map/while/body/eval_jaxpr/ppermute | solution.py:13
  289.8 11.5 %collective-permute-done = f32[16,64,64]{2,1,0:T(8,128)S(1)} collective-permute-done((f32[16,64,64]{2,1,0:T(8,128)}, f32[16,64,64]{2,1,0:T(8,128)S(1)}, u32[]{:S(2)}, u32[]{:S(2)}) %collective-permute-start) | collective-permute-done | bytes 262176 | tf_op jit(solution)/shard_map/while/body/eval_jaxpr/ppermute | solution.py:13
  304.1 15.8 %while.75 = (s32[]{:T(128)}, f32[16,64,64]{2,1,0:T(8,128)S(1)}, bf16[2,16,64,64]{3,2,1,0:T(8,128)(2,1)}, f32[2,16,64,64]{2,3,1,0:T(8,128)S(1)}, f32[2,16,64]{2,1...) while((s32[]{:T(128)}, f32[16,64,64]{2,1,0:T(8,128)S(1)}, ...), condition=%wide.region_8.9_spmd, body=%wide.region_7.8_spmd.sunk | while | flops 251994112 | bytes 10029721 | solution.py:108
  357.0 268.0 %while.76 = (s32[]{:T(128)}, f32[16,64,64]{2,1,0:T(8,128)S(1)}, pred[]{:T(512)}, f32[16,64,64]{2,1,0:T(8,128)S(1)}, f32[16,64,64]{2,1,0:T(8,128)}, /*index=5*/f32[16,64,64]{2,1,0:T(8,128)S(1)}, s32[]{:T(128)}) while((s32[]{:T(128)}, f32[16,64,64]{2,1,0:T(8,128)S(1)}, pred[]{:T(512)}, f32[16,64,64]{2,1,0:T(8,128)S(1)}, ...), condition=%wide.region_14.15_spmd, body=%wide.region_13.14_spmd.sunk | while | flops 50462720 | bytes 2883702 | solution.py:107
  361.4 16.5 %collective-permute-done.1 = f32[16,64,64]{2,1,0:T(8,128)S(1)} collective-permute-done((f32[16,64,64]{2,1,0:T(8,128)}, f32[16,64,64]{2,1,0:T(8,128)S(1)}, u32[]{:S(2)}, u32[]{:S(2)}) %collective-permute-start.1) | collective-permute-done | bytes 262176 | tf_op jit(solution)/shard_map/while/body/eval_jaxpr/ppermute | solution.py:13
  382.4 15.7 %collective-permute-done.1 = f32[16,64,64]{2,1,0:T(8,128)S(1)} collective-permute-done((f32[16,64,64]{2,1,0:T(8,128)}, f32[16,64,64]{2,1,0:T(8,128)S(1)}, u32[]{:S(2)}, u32[]{:S(2)}) %collective-permute-start.1) | collective-permute-done | bytes 262176 | tf_op jit(solution)/shard_map/while/body/eval_jaxpr/ppermute | solution.py:13
  402.5 14.8 %collective-permute-done.1 = f32[16,64,64]{2,1,0:T(8,128)S(1)} collective-permute-done((f32[16,64,64]{2,1,0:T(8,128)}, f32[16,64,64]{2,1,0:T(8,128)S(1)}, u32[]{:S(2)}, u32[]{:S(2)}) %collective-permute-start.1) | collective-permute-done | bytes 262176 | tf_op jit(solution)/shard_map/while/body/eval_jaxpr/ppermute | solution.py:13
  421.8 13.8 %collective-permute-done.1 = f32[16,64,64]{2,1,0:T(8,128)S(1)} collective-permute-done((f32[16,64,64]{2,1,0:T(8,128)}, f32[16,64,64]{2,1,0:T(8,128)S(1)}, u32[]{:S(2)}, u32[]{:S(2)}) %collective-permute-start.1) | collective-permute-done | bytes 262176 | tf_op jit(solution)/shard_map/while/body/eval_jaxpr/ppermute | solution.py:13
  440.1 12.9 %collective-permute-done.1 = f32[16,64,64]{2,1,0:T(8,128)S(1)} collective-permute-done((f32[16,64,64]{2,1,0:T(8,128)}, f32[16,64,64]{2,1,0:T(8,128)S(1)}, u32[]{:S(2)}, u32[]{:S(2)}) %collective-permute-start.1) | collective-permute-done | bytes 262176 | tf_op jit(solution)/shard_map/while/body/eval_jaxpr/ppermute | solution.py:13
  457.5 12.0 %collective-permute-done.1 = f32[16,64,64]{2,1,0:T(8,128)S(1)} collective-permute-done((f32[16,64,64]{2,1,0:T(8,128)}, f32[16,64,64]{2,1,0:T(8,128)S(1)}, u32[]{:S(2)}, u32[]{:S(2)}) %collective-permute-start.1) | collective-permute-done | bytes 262176 | tf_op jit(solution)/shard_map/while/body/eval_jaxpr/ppermute | solution.py:13
  474.0 11.5 %collective-permute-done.1 = f32[16,64,64]{2,1,0:T(8,128)S(1)} collective-permute-done((f32[16,64,64]{2,1,0:T(8,128)}, f32[16,64,64]{2,1,0:T(8,128)S(1)}, u32[]{:S(2)}, u32[]{:S(2)}) %collective-permute-start.1) | collective-permute-done | bytes 262176 | tf_op jit(solution)/shard_map/while/body/eval_jaxpr/ppermute | solution.py:13
  489.9 11.5 %collective-permute-done.1 = f32[16,64,64]{2,1,0:T(8,128)S(1)} collective-permute-done((f32[16,64,64]{2,1,0:T(8,128)}, f32[16,64,64]{2,1,0:T(8,128)S(1)}, u32[]{:S(2)}, u32[]{:S(2)}) %collective-permute-start.1) | collective-permute-done | bytes 262176 | tf_op jit(solution)/shard_map/while/body/eval_jaxpr/ppermute | solution.py:13
  505.9 11.5 %collective-permute-done.1 = f32[16,64,64]{2,1,0:T(8,128)S(1)} collective-permute-done((f32[16,64,64]{2,1,0:T(8,128)}, f32[16,64,64]{2,1,0:T(8,128)S(1)}, u32[]{:S(2)}, u32[]{:S(2)}) %collective-permute-start.1) | collective-permute-done | bytes 262176 | tf_op jit(solution)/shard_map/while/body/eval_jaxpr/ppermute | solution.py:13
  521.8 11.7 %collective-permute-done.1 = f32[16,64,64]{2,1,0:T(8,128)S(1)} collective-permute-done((f32[16,64,64]{2,1,0:T(8,128)}, f32[16,64,64]{2,1,0:T(8,128)S(1)}, u32[]{:S(2)}, u32[]{:S(2)}) %collective-permute-start.1) | collective-permute-done | bytes 262176 | tf_op jit(solution)/shard_map/while/body/eval_jaxpr/ppermute | solution.py:13
  538.0 12.8 %collective-permute-done.1 = f32[16,64,64]{2,1,0:T(8,128)S(1)} collective-permute-done((f32[16,64,64]{2,1,0:T(8,128)}, f32[16,64,64]{2,1,0:T(8,128)S(1)}, u32[]{:S(2)}, u32[]{:S(2)}) %collective-permute-start.1) | collective-permute-done | bytes 262176 | tf_op jit(solution)/shard_map/while/body/eval_jaxpr/ppermute | solution.py:13
  555.2 13.8 %collective-permute-done.1 = f32[16,64,64]{2,1,0:T(8,128)S(1)} collective-permute-done((f32[16,64,64]{2,1,0:T(8,128)}, f32[16,64,64]{2,1,0:T(8,128)S(1)}, u32[]{:S(2)}, u32[]{:S(2)}) %collective-permute-start.1) | collective-permute-done | bytes 262176 | tf_op jit(solution)/shard_map/while/body/eval_jaxpr/ppermute | solution.py:13
  573.6 14.9 %collective-permute-done.1 = f32[16,64,64]{2,1,0:T(8,128)S(1)} collective-permute-done((f32[16,64,64]{2,1,0:T(8,128)}, f32[16,64,64]{2,1,0:T(8,128)S(1)}, u32[]{:S(2)}, u32[]{:S(2)}) %collective-permute-start.1) | collective-permute-done | bytes 262176 | tf_op jit(solution)/shard_map/while/body/eval_jaxpr/ppermute | solution.py:13
  593.0 16.1 %collective-permute-done.1 = f32[16,64,64]{2,1,0:T(8,128)S(1)} collective-permute-done((f32[16,64,64]{2,1,0:T(8,128)}, f32[16,64,64]{2,1,0:T(8,128)S(1)}, u32[]{:S(2)}, u32[]{:S(2)}) %collective-permute-start.1) | collective-permute-done | bytes 262176 | tf_op jit(solution)/shard_map/while/body/eval_jaxpr/ppermute | solution.py:13
  613.5 11.5 %collective-permute-done.1 = f32[16,64,64]{2,1,0:T(8,128)S(1)} collective-permute-done((f32[16,64,64]{2,1,0:T(8,128)}, f32[16,64,64]{2,1,0:T(8,128)S(1)}, u32[]{:S(2)}, u32[]{:S(2)}) %collective-permute-start.1) | collective-permute-done | bytes 262176 | tf_op jit(solution)/shard_map/while/body/eval_jaxpr/ppermute | solution.py:13
  625.2 14.2 %while.77 = (s32[]{:T(128)}, f32[16,64,64]{2,1,0:T(8,128)S(1)}, bf16[2,16,64,64]{3,2,1,0:T(8,128)(2,1)S(1)}, f32[2,16,64,64]{2,3,1,0:T(8,128)S(1)}, f32[2,16,64]...) while((s32[]{:T(128)}, f32[16,64,64]{2,1,0:T(8,128)S(1)}, ...), condition=%wide.region_17.18_spmd, body=%wide.region_16.17_spmd.sunk | while | flops 251994112 | bytes 7932513 | solution.py:108
  (270 shorter events, 287.4 us)
Async XLA Ops:
  28.0 17.9 %collective-permute-start = (f32[16,64,64]{2,1,0:T(8,128)}, f32[16,64,64]{2,1,0:T(8,128)S(1)}, u32[]{:S(2)}, u32[]{:S(2)}) collective-permute-start(f32[16,64,64]{2,1,0:T(8,128)} %convolution_add_fusion.8), channel_id=1, source_target_pairs={{0,8},{8,16},{16,24},{24,32},{32,40},{40,48},{48,56},{56,64},{64,7... | collective-permute-start | bytes 786440 | tf_op jit(solution)/shard_map/while/body/eval_jaxpr/ppermute | solution.py:13
  49.3 17.0 %collective-permute-start = (f32[16,64,64]{2,1,0:T(8,128)}, f32[16,64,64]{2,1,0:T(8,128)S(1)}, u32[]{:S(2)}, u32[]{:S(2)}) collective-permute-start(f32[16,64,64]{2,1,0:T(8,128)} %convolution_add_fusion.8), channel_id=1, source_target_pairs={{0,8},{8,16},{16,24},{24,32},{32,40},{40,48},{48,56},{56,64},{64,7... | collective-permute-start | bytes 786440 | tf_op jit(solution)/shard_map/while/body/eval_jaxpr/ppermute | solution.py:13
  69.6 16.1 %collective-permute-start = (f32[16,64,64]{2,1,0:T(8,128)}, f32[16,64,64]{2,1,0:T(8,128)S(1)}, u32[]{:S(2)}, u32[]{:S(2)}) collective-permute-start(f32[16,64,64]{2,1,0:T(8,128)} %convolution_add_fusion.8), channel_id=1, source_target_pairs={{0,8},{8,16},{16,24},{24,32},{32,40},{40,48},{48,56},{56,64},{64,7... | collective-permute-start | bytes 786440 | tf_op jit(solution)/shard_map/while/body/eval_jaxpr/ppermute | solution.py:13
  89.0 15.2 %collective-permute-start = (f32[16,64,64]{2,1,0:T(8,128)}, f32[16,64,64]{2,1,0:T(8,128)S(1)}, u32[]{:S(2)}, u32[]{:S(2)}) collective-permute-start(f32[16,64,64]{2,1,0:T(8,128)} %convolution_add_fusion.8), channel_id=1, source_target_pairs={{0,8},{8,16},{16,24},{24,32},{32,40},{40,48},{48,56},{56,64},{64,7... | collective-permute-start | bytes 786440 | tf_op jit(solution)/shard_map/while/body/eval_jaxpr/ppermute | solution.py:13
  107.5 14.2 %collective-permute-start = (f32[16,64,64]{2,1,0:T(8,128)}, f32[16,64,64]{2,1,0:T(8,128)S(1)}, u32[]{:S(2)}, u32[]{:S(2)}) collective-permute-start(f32[16,64,64]{2,1,0:T(8,128)} %convolution_add_fusion.8), channel_id=1, source_target_pairs={{0,8},{8,16},{16,24},{24,32},{32,40},{40,48},{48,56},{56,64},{64,7... | collective-permute-start | bytes 786440 | tf_op jit(solution)/shard_map/while/body/eval_jaxpr/ppermute | solution.py:13
  125.1 13.4 %collective-permute-start = (f32[16,64,64]{2,1,0:T(8,128)}, f32[16,64,64]{2,1,0:T(8,128)S(1)}, u32[]{:S(2)}, u32[]{:S(2)}) collective-permute-start(f32[16,64,64]{2,1,0:T(8,128)} %convolution_add_fusion.8), channel_id=1, source_target_pairs={{0,8},{8,16},{16,24},{24,32},{32,40},{40,48},{48,56},{56,64},{64,7... | collective-permute-start | bytes 786440 | tf_op jit(solution)/shard_map/while/body/eval_jaxpr/ppermute | solution.py:13
  141.9 13.4 %collective-permute-start = (f32[16,64,64]{2,1,0:T(8,128)}, f32[16,64,64]{2,1,0:T(8,128)S(1)}, u32[]{:S(2)}, u32[]{:S(2)}) collective-permute-start(f32[16,64,64]{2,1,0:T(8,128)} %convolution_add_fusion.8), channel_id=1, source_target_pairs={{0,8},{8,16},{16,24},{24,32},{32,40},{40,48},{48,56},{56,64},{64,7... | collective-permute-start | bytes 786440 | tf_op jit(solution)/shard_map/while/body/eval_jaxpr/ppermute | solution.py:13
  158.6 13.4 %collective-permute-start = (f32[16,64,64]{2,1,0:T(8,128)}, f32[16,64,64]{2,1,0:T(8,128)S(1)}, u32[]{:S(2)}, u32[]{:S(2)}) collective-permute-start(f32[16,64,64]{2,1,0:T(8,128)} %convolution_add_fusion.8), channel_id=1, source_target_pairs={{0,8},{8,16},{16,24},{24,32},{32,40},{40,48},{48,56},{56,64},{64,7... | collective-permute-start | bytes 786440 | tf_op jit(solution)/shard_map/while/body/eval_jaxpr/ppermute | solution.py:13
  175.3 13.4 %collective-permute-start = (f32[16,64,64]{2,1,0:T(8,128)}, f32[16,64,64]{2,1,0:T(8,128)S(1)}, u32[]{:S(2)}, u32[]{:S(2)}) collective-permute-start(f32[16,64,64]{2,1,0:T(8,128)} %convolution_add_fusion.8), channel_id=1, source_target_pairs={{0,8},{8,16},{16,24},{24,32},{32,40},{40,48},{48,56},{56,64},{64,7... | collective-permute-start | bytes 786440 | tf_op jit(solution)/shard_map/while/body/eval_jaxpr/ppermute | solution.py:13
  192.1 13.6 %collective-permute-start = (f32[16,64,64]{2,1,0:T(8,128)}, f32[16,64,64]{2,1,0:T(8,128)S(1)}, u32[]{:S(2)}, u32[]{:S(2)}) collective-permute-start(f32[16,64,64]{2,1,0:T(8,128)} %convolution_add_fusion.8), channel_id=1, source_target_pairs={{0,8},{8,16},{16,24},{24,32},{32,40},{40,48},{48,56},{56,64},{64,7... | collective-permute-start | bytes 786440 | tf_op jit(solution)/shard_map/while/body/eval_jaxpr/ppermute | solution.py:13
  209.1 14.7 %collective-permute-start = (f32[16,64,64]{2,1,0:T(8,128)}, f32[16,64,64]{2,1,0:T(8,128)S(1)}, u32[]{:S(2)}, u32[]{:S(2)}) collective-permute-start(f32[16,64,64]{2,1,0:T(8,128)} %convolution_add_fusion.8), channel_id=1, source_target_pairs={{0,8},{8,16},{16,24},{24,32},{32,40},{40,48},{48,56},{56,64},{64,7... | collective-permute-start | bytes 786440 | tf_op jit(solution)/shard_map/while/body/eval_jaxpr/ppermute | solution.py:13
  227.1 15.8 %collective-permute-start = (f32[16,64,64]{2,1,0:T(8,128)}, f32[16,64,64]{2,1,0:T(8,128)S(1)}, u32[]{:S(2)}, u32[]{:S(2)}) collective-permute-start(f32[16,64,64]{2,1,0:T(8,128)} %convolution_add_fusion.8), channel_id=1, source_target_pairs={{0,8},{8,16},{16,24},{24,32},{32,40},{40,48},{48,56},{56,64},{64,7... | collective-permute-start | bytes 786440 | tf_op jit(solution)/shard_map/while/body/eval_jaxpr/ppermute | solution.py:13
  246.3 16.9 %collective-permute-start = (f32[16,64,64]{2,1,0:T(8,128)}, f32[16,64,64]{2,1,0:T(8,128)S(1)}, u32[]{:S(2)}, u32[]{:S(2)}) collective-permute-start(f32[16,64,64]{2,1,0:T(8,128)} %convolution_add_fusion.8), channel_id=1, source_target_pairs={{0,8},{8,16},{16,24},{24,32},{32,40},{40,48},{48,56},{56,64},{64,7... | collective-permute-start | bytes 786440 | tf_op jit(solution)/shard_map/while/body/eval_jaxpr/ppermute | solution.py:13
  266.5 18.0 %collective-permute-start = (f32[16,64,64]{2,1,0:T(8,128)}, f32[16,64,64]{2,1,0:T(8,128)S(1)}, u32[]{:S(2)}, u32[]{:S(2)}) collective-permute-start(f32[16,64,64]{2,1,0:T(8,128)} %convolution_add_fusion.8), channel_id=1, source_target_pairs={{0,8},{8,16},{16,24},{24,32},{32,40},{40,48},{48,56},{56,64},{64,7... | collective-permute-start | bytes 786440 | tf_op jit(solution)/shard_map/while/body/eval_jaxpr/ppermute | solution.py:13
  287.9 13.4 %collective-permute-start = (f32[16,64,64]{2,1,0:T(8,128)}, f32[16,64,64]{2,1,0:T(8,128)S(1)}, u32[]{:S(2)}, u32[]{:S(2)}) collective-permute-start(f32[16,64,64]{2,1,0:T(8,128)} %convolution_add_fusion.8), channel_id=1, source_target_pairs={{0,8},{8,16},{16,24},{24,32},{32,40},{40,48},{48,56},{56,64},{64,7... | collective-permute-start | bytes 786440 | tf_op jit(solution)/shard_map/while/body/eval_jaxpr/ppermute | solution.py:13
  304.1 17.6 %copy-start.6 = (bf16[128,2048]{1,0:T(8,128)(2,1)S(1)}, bf16[128,2048]{1,0:T(8,128)(2,1)}, u32[]{:S(2)}) copy-start(bf16[128,2048]{1,0:T(8,128)(2,1)} %param.19) | copy-start | bytes 1572868
  324.6 2.8 collective-permute-start.2
  359.5 18.4 %collective-permute-start.1 = (f32[16,64,64]{2,1,0:T(8,128)}, f32[16,64,64]{2,1,0:T(8,128)S(1)}, u32[]{:S(2)}, u32[]{:S(2)}) collective-permute-start(f32[16,64,64]{2,1,0:T(8,128)} %convolution_add_fusion.9), channel_id=1, source_target_pairs={{0,8},{8,16},{16,24},{24,32},{32,40},{40,48},{48,56},{56,64},{64,7... | collective-permute-start | bytes 786440 | tf_op jit(solution)/shard_map/while/body/eval_jaxpr/ppermute | solution.py:13
  380.5 17.6 %collective-permute-start.1 = (f32[16,64,64]{2,1,0:T(8,128)}, f32[16,64,64]{2,1,0:T(8,128)S(1)}, u32[]{:S(2)}, u32[]{:S(2)}) collective-permute-start(f32[16,64,64]{2,1,0:T(8,128)} %convolution_add_fusion.9), channel_id=1, source_target_pairs={{0,8},{8,16},{16,24},{24,32},{32,40},{40,48},{48,56},{56,64},{64,7... | collective-permute-start | bytes 786440 | tf_op jit(solution)/shard_map/while/body/eval_jaxpr/ppermute | solution.py:13
  400.6 16.7 %collective-permute-start.1 = (f32[16,64,64]{2,1,0:T(8,128)}, f32[16,64,64]{2,1,0:T(8,128)S(1)}, u32[]{:S(2)}, u32[]{:S(2)}) collective-permute-start(f32[16,64,64]{2,1,0:T(8,128)} %convolution_add_fusion.9), channel_id=1, source_target_pairs={{0,8},{8,16},{16,24},{24,32},{32,40},{40,48},{48,56},{56,64},{64,7... | collective-permute-start | bytes 786440 | tf_op jit(solution)/shard_map/while/body/eval_jaxpr/ppermute | solution.py:13
  419.8 15.7 %collective-permute-start.1 = (f32[16,64,64]{2,1,0:T(8,128)}, f32[16,64,64]{2,1,0:T(8,128)S(1)}, u32[]{:S(2)}, u32[]{:S(2)}) collective-permute-start(f32[16,64,64]{2,1,0:T(8,128)} %convolution_add_fusion.9), channel_id=1, source_target_pairs={{0,8},{8,16},{16,24},{24,32},{32,40},{40,48},{48,56},{56,64},{64,7... | collective-permute-start | bytes 786440 | tf_op jit(solution)/shard_map/while/body/eval_jaxpr/ppermute | solution.py:13
  438.2 14.8 %collective-permute-start.1 = (f32[16,64,64]{2,1,0:T(8,128)}, f32[16,64,64]{2,1,0:T(8,128)S(1)}, u32[]{:S(2)}, u32[]{:S(2)}) collective-permute-start(f32[16,64,64]{2,1,0:T(8,128)} %convolution_add_fusion.9), channel_id=1, source_target_pairs={{0,8},{8,16},{16,24},{24,32},{32,40},{40,48},{48,56},{56,64},{64,7... | collective-permute-start | bytes 786440 | tf_op jit(solution)/shard_map/while/body/eval_jaxpr/ppermute | solution.py:13
  455.6 13.9 %collective-permute-start.1 = (f32[16,64,64]{2,1,0:T(8,128)}, f32[16,64,64]{2,1,0:T(8,128)S(1)}, u32[]{:S(2)}, u32[]{:S(2)}) collective-permute-start(f32[16,64,64]{2,1,0:T(8,128)} %convolution_add_fusion.9), channel_id=1, source_target_pairs={{0,8},{8,16},{16,24},{24,32},{32,40},{40,48},{48,56},{56,64},{64,7... | collective-permute-start | bytes 786440 | tf_op jit(solution)/shard_map/while/body/eval_jaxpr/ppermute | solution.py:13
  472.0 13.4 %collective-permute-start.1 = (f32[16,64,64]{2,1,0:T(8,128)}, f32[16,64,64]{2,1,0:T(8,128)S(1)}, u32[]{:S(2)}, u32[]{:S(2)}) collective-permute-start(f32[16,64,64]{2,1,0:T(8,128)} %convolution_add_fusion.9), channel_id=1, source_target_pairs={{0,8},{8,16},{16,24},{24,32},{32,40},{40,48},{48,56},{56,64},{64,7... | collective-permute-start | bytes 786440 | tf_op jit(solution)/shard_map/while/body/eval_jaxpr/ppermute | solution.py:13
  488.0 13.4 %collective-permute-start.1 = (f32[16,64,64]{2,1,0:T(8,128)}, f32[16,64,64]{2,1,0:T(8,128)S(1)}, u32[]{:S(2)}, u32[]{:S(2)}) collective-permute-start(f32[16,64,64]{2,1,0:T(8,128)} %convolution_add_fusion.9), channel_id=1, source_target_pairs={{0,8},{8,16},{16,24},{24,32},{32,40},{40,48},{48,56},{56,64},{64,7... | collective-permute-start | bytes 786440 | tf_op jit(solution)/shard_map/while/body/eval_jaxpr/ppermute | solution.py:13
  503.9 13.4 %collective-permute-start.1 = (f32[16,64,64]{2,1,0:T(8,128)}, f32[16,64,64]{2,1,0:T(8,128)S(1)}, u32[]{:S(2)}, u32[]{:S(2)}) collective-permute-start(f32[16,64,64]{2,1,0:T(8,128)} %convolution_add_fusion.9), channel_id=1, source_target_pairs={{0,8},{8,16},{16,24},{24,32},{32,40},{40,48},{48,56},{56,64},{64,7... | collective-permute-start | bytes 786440 | tf_op jit(solution)/shard_map/while/body/eval_jaxpr/ppermute | solution.py:13
  519.9 13.6 %collective-permute-start.1 = (f32[16,64,64]{2,1,0:T(8,128)}, f32[16,64,64]{2,1,0:T(8,128)S(1)}, u32[]{:S(2)}, u32[]{:S(2)}) collective-permute-start(f32[16,64,64]{2,1,0:T(8,128)} %convolution_add_fusion.9), channel_id=1, source_target_pairs={{0,8},{8,16},{16,24},{24,32},{32,40},{40,48},{48,56},{56,64},{64,7... | collective-permute-start | bytes 786440 | tf_op jit(solution)/shard_map/while/body/eval_jaxpr/ppermute | solution.py:13
  536.1 14.7 %collective-permute-start.1 = (f32[16,64,64]{2,1,0:T(8,128)}, f32[16,64,64]{2,1,0:T(8,128)S(1)}, u32[]{:S(2)}, u32[]{:S(2)}) collective-permute-start(f32[16,64,64]{2,1,0:T(8,128)} %convolution_add_fusion.9), channel_id=1, source_target_pairs={{0,8},{8,16},{16,24},{24,32},{32,40},{40,48},{48,56},{56,64},{64,7... | collective-permute-start | bytes 786440 | tf_op jit(solution)/shard_map/while/body/eval_jaxpr/ppermute | solution.py:13
  553.3 15.8 %collective-permute-start.1 = (f32[16,64,64]{2,1,0:T(8,128)}, f32[16,64,64]{2,1,0:T(8,128)S(1)}, u32[]{:S(2)}, u32[]{:S(2)}) collective-permute-start(f32[16,64,64]{2,1,0:T(8,128)} %convolution_add_fusion.9), channel_id=1, source_target_pairs={{0,8},{8,16},{16,24},{24,32},{32,40},{40,48},{48,56},{56,64},{64,7... | collective-permute-start | bytes 786440 | tf_op jit(solution)/shard_map/while/body/eval_jaxpr/ppermute | solution.py:13
  571.6 16.8 %collective-permute-start.1 = (f32[16,64,64]{2,1,0:T(8,128)}, f32[16,64,64]{2,1,0:T(8,128)S(1)}, u32[]{:S(2)}, u32[]{:S(2)}) collective-permute-start(f32[16,64,64]{2,1,0:T(8,128)} %convolution_add_fusion.9), channel_id=1, source_target_pairs={{0,8},{8,16},{16,24},{24,32},{32,40},{40,48},{48,56},{56,64},{64,7... | collective-permute-start | bytes 786440 | tf_op jit(solution)/shard_map/while/body/eval_jaxpr/ppermute | solution.py:13
  591.1 18.0 %collective-permute-start.1 = (f32[16,64,64]{2,1,0:T(8,128)}, f32[16,64,64]{2,1,0:T(8,128)S(1)}, u32[]{:S(2)}, u32[]{:S(2)}) collective-permute-start(f32[16,64,64]{2,1,0:T(8,128)} %convolution_add_fusion.9), channel_id=1, source_target_pairs={{0,8},{8,16},{16,24},{24,32},{32,40},{40,48},{48,56},{56,64},{64,7... | collective-permute-start | bytes 786440 | tf_op jit(solution)/shard_map/while/body/eval_jaxpr/ppermute | solution.py:13
  611.6 13.4 %collective-permute-start.1 = (f32[16,64,64]{2,1,0:T(8,128)}, f32[16,64,64]{2,1,0:T(8,128)S(1)}, u32[]{:S(2)}, u32[]{:S(2)}) collective-permute-start(f32[16,64,64]{2,1,0:T(8,128)} %convolution_add_fusion.9), channel_id=1, source_target_pairs={{0,8},{8,16},{16,24},{24,32},{32,40},{40,48},{48,56},{56,64},{64,7... | collective-permute-start | bytes 786440 | tf_op jit(solution)/shard_map/while/body/eval_jaxpr/ppermute | solution.py:13
  (27 other events, 93.6 us)
where the time goes:
time: 648 us; the launch traced here: 644 us
  waiting for transfers between devices  398 us (61%)
  matrix products  126 us (19%)
  starting transfers between devices  60.3 us (9%)
  local copies, waits for them, and re-layouts  29.6 us (5%)
  other arithmetic  27.7 us (4%)
    ppermute x31, waiting for transfers between devices, from_behind(): lax.ppermute(value, axis, [(source, source + steps) for source in range(i...  398 us
    dot_general x34, matrix products, apply_map(): jnp.einsum('hde,hef->hdf', linear_output, weight_state, precision=lax.Pre...  62.7 us
    ppermute x31, starting transfers between devices, from_behind(): lax.ppermute(value, axis, [(source, source + steps) for source in range(i...  60.3 us
    select_n x30, other arithmetic, relay(): return jnp.where(seq_index == 0, init_state, received)  17.4 us
    while x42, local copies, waits for them, and re-layouts  13.6 us
    dot_general x2, matrix products, inner_inputs(): projected = jnp.dot(normed, w_qkv, preferred_element_type=jnp.float32)  13.2 us
  transfers between devices with their start and end apart: 31, of which 31 were waited for; matrix products, arithmetic and copies ran while one was open for 0% of the time, Pallas kernels for 0%

commit v1 on v0

v1 whole, which is shorter than its diff:
```python
import jax
import jax.numpy as jnp
from jax import lax
from jax.experimental import pallas as pl
from jax.experimental.pallas import tpu as pltpu
from jax.sharding import PartitionSpec as P

HD = 64
MB = 64
PAIR = 2 * HD
GROUP = 4 * HD
EPS = 1e-06
MESH = pl.DeviceIdType.MESH
F32 = jnp.float32
BF16 = jnp.bfloat16


def dot(a, b, dims=((1,), (0,))):
    return lax.dot_general(a, b, (dims, ((), ())), preferred_element_type=F32)


def split(x):
    high = x.astype(BF16)
    return high, (x - high.astype(F32)).astype(BF16)


def iota(shape, axis):
    return lax.broadcasted_iota(jnp.int32, shape, axis)


def head_ones():
    same = iota((GROUP, GROUP), 0) // HD == iota((GROUP, GROUP), 1) // HD
    return jnp.where(same, 1.0, 0.0).astype(BF16)


def unit_rows(x, ones):
    high, low = split(x * x)
    return x * lax.rsqrt(dot(high, ones) + dot(low, ones) + EPS)


def kernel(
    seq_count,
    tok, gain, w_qkv, w_rate, rate_base, init_state, w_out,
    out,
    hidden, gain_v, wkv_v, wq_v, wrate_v, rbase_v, wout_v, init_v,
    normed, rate_hl, keys, scaled, first_map, sent_map, got_map, sent_state, got_state,
    query_map, offset, inner, result,
    load_sem, weight_sem, out_sem,
    map_send, map_recv, state_send, state_recv, hid_send, hid_recv,
):
    section = lax.axis_index("section")
    me = lax.axis_index("seq")
    rows, width = tok.shape
    heads = rate_base.shape[1]
    inner_width = heads * HD
    groups = inner_width // GROUP
    chunks = hid_send.shape[0]
    chunk = width // chunks

    token_copy = pltpu.make_async_copy(tok, hidden, load_sem.at[0])

    @pl.when(section == 0)
    def _():
        token_copy.start()

    small = [
        pltpu.make_async_copy(gain, gain_v, load_sem.at[1]),
        pltpu.make_async_copy(w_rate.at[0], wrate_v, load_sem.at[2]),
        pltpu.make_async_copy(rate_base, rbase_v, load_sem.at[3]),
        pltpu.make_async_copy(init_state.at[0, me], init_v, load_sem.at[4]),
    ]
    for copy in small:
        copy.start()

    def key_copy(g):
        return pltpu.make_async_copy(
            w_qkv.at[0, :, pl.ds(pl.multiple_of(inner_width + g * GROUP, GROUP), GROUP)],
            wkv_v.at[g, :, pl.ds(0, GROUP)], weight_sem.at[0, g])

    def value_copy(g):
        return pltpu.make_async_copy(
            w_qkv.at[0, :, pl.ds(pl.multiple_of(2 * inner_width + g * GROUP, GROUP), GROUP)],
            wkv_v.at[g, :, pl.ds(GROUP, GROUP)], weight_sem.at[1, g])

    def query_copy(g):
        return pltpu.make_async_copy(
            w_qkv.at[0, :, pl.ds(pl.multiple_of(g * GROUP, GROUP), GROUP)],
            wq_v.at[g], weight_sem.at[2, g])

    def out_weight_copy(n):
        return pltpu.make_async_copy(
            w_out.at[0, :, pl.ds(pl.multiple_of(n * chunk, chunk), chunk)],
            wout_v.at[n], weight_sem.at[3, n])

    for g in range(groups):
        key_copy(g).start()
        value_copy(g).start()
    for g in range(groups):
        query_copy(g).start()
    for n in range(chunks):
        out_weight_copy(n).start()

    barrier = pltpu.get_barrier_semaphore()
    for step in range(1, seq_count):
        pl.semaphore_signal(
            barrier, inc=1, device_id={"seq": lax.rem(me + step, seq_count)}, device_id_type=MESH)
    pl.semaphore_signal(barrier, inc=1, device_id={"section": 1 - section}, device_id_type=MESH)
    pl.semaphore_wait(barrier, seq_count)

    def hidden_copy(n):
        piece = pl.ds(pl.multiple_of(n * chunk, chunk), chunk)
        return pltpu.make_async_remote_copy(
            src_ref=result.at[:, piece], dst_ref=hidden.at[:, piece],
            send_sem=hid_send.at[n], recv_sem=hid_recv.at[n],
            device_id={"section": 1 - section}, device_id_type=MESH)

    def result_copy(n):
        piece = pl.ds(pl.multiple_of(n * chunk, chunk), chunk)
        return pltpu.make_async_copy(result.at[:, piece], out.at[0, :, piece], out_sem.at[n])

    @pl.when(section == 0)
    def _():
        token_copy.wait()

    for copy in small:
        copy.wait()

    @pl.when(section == 1)
    def _():
        for n in range(chunks):
            hidden_copy(n).wait_recv()

    wide = hidden[...].astype(F32)
    mean_sq = jnp.mean(wide * wide, axis=-1, keepdims=True)
    normed[...] = (wide * lax.rsqrt(mean_sq + EPS) * gain_v[...]).astype(BF16)
    rates = rbase_v[...] * jax.nn.sigmoid(dot(normed[...], wrate_v[...], ((1,), (1,))))
    high, low = split(rates)
    rate_hl[0] = high
    rate_hl[1] = low

    lane_low = iota((MB, PAIR), 1) < HD
    diagonal = iota((PAIR, 2 * PAIR), 0) // HD == (iota((PAIR, 2 * PAIR), 1) % PAIR) // HD

    def map_copy(h):
        return pltpu.make_async_remote_copy(
            src_ref=sent_map.at[h], dst_ref=got_map.at[me],
            send_sem=map_send.at[h], recv_sem=map_recv.at[me],
            device_id={"seq": h}, device_id_type=MESH)

    def key_group(g, carry):
        key_copy(g).wait()
        value_copy(g).wait()
        ones = head_ones()
        both = dot(normed[...], wkv_v[g])
        key = unit_rows(both[:, :GROUP], ones)
        spread = jnp.where(
            iota((heads, GROUP), 0) == 4 * g + iota((heads, GROUP), 1) // HD, 1.0, 0.0).astype(BF16)
        rate = dot(rate_hl[0], spread) + dot(rate_hl[1], spread)
        key_bf = key.astype(BF16)
        rated_key = (rate * key).astype(BF16)
        rated_value = (rate * both[:, GROUP:]).astype(BF16)
        for i in range(2):
            lanes = slice(i * PAIR, (i + 1) * PAIR)
            pair = 2 * g + i
            pair_key = key_bf[:, lanes]
            pair_scaled = jnp.concatenate([rated_value[:, lanes], rated_key[:, lanes]], axis=1)
            keys[pair] = pair_key
            scaled[pair] = pair_scaled
            first = jnp.where(diagonal, dot(pair_key[:MB], pair_scaled[:MB], ((0,), (0,))), 0.0)
            second = jnp.where(diagonal, dot(pair_key[MB:], pair_scaled[MB:], ((0,), (0,))), 0.0)
            first_bf = first.astype(BF16)
            first_map[pair] = first_bf
            total = first + second - dot(second[:, PAIR:].astype(BF16), first_bf)
            packed = total[:HD] + total[HD:]
            pack_b, pack_d = packed[:, :PAIR], packed[:, PAIR:]
            even = jnp.where(lane_low, pack_b, pltpu.roll(pack_d, HD, 1)).astype(BF16)
            odd = jnp.where(lane_low, pltpu.roll(pack_b, HD, 1), pack_d).astype(BF16)
            for parity, message in enumerate((even, odd)):
                h = 2 * pair + parity
                sent_map[h] = message

                @pl.when(h == me)
                def _():
                    got_map[me] = message

                @pl.when(h != me)
                def _():
                    map_copy(h).start()

        return carry

    lax.fori_loop(0, groups, key_group, 0)

    row = iota((4 * MB, PAIR), 0)
    column = iota((4 * MB, PAIR), 1)
    causal = (column // MB == row // PAIR) & (column % MB <= row % MB)
    low_half = iota((MB, 2 * PAIR), 1) % PAIR < HD

    def query_group(g, carry):
        query_copy(g).wait()
        query_all = unit_rows(dot(normed[...], wq_v[g]), head_ones())
        for i in range(2):
            pair = 2 * g + i
            query = query_all[:, i * PAIR:(i + 1) * PAIR]
            parts = []
            for b in range(2):
                piece = query[b * MB:(b + 1) * MB]
                parts += [jnp.where(lane_low, piece, 0.0), jnp.where(lane_low, 0.0, piece)]
            stacked = jnp.concatenate(parts, axis=0).astype(BF16)
            scores = jnp.where(causal, dot(stacked, keys[pair], ((1,), (1,))), 0.0).astype(BF16)
            mixed = dot(scores, scaled[pair])
            mix_one = jnp.where(low_half, mixed[:MB], mixed[MB:2 * MB])
            mix_two = jnp.where(low_half, mixed[2 * MB:3 * MB], mixed[3 * MB:])
            map_one = query[:MB] - mix_one[:, PAIR:]
            map_two = query[MB:] - mix_two[:, PAIR:]
            through = dot(map_two.astype(BF16), first_map[pair])
            query_map[pair, pl.ds(0, MB), :] = map_one.astype(BF16)
            query_map[pair, pl.ds(MB, MB), :] = (map_two - through[:, PAIR:]).astype(BF16)
            offset[pair, pl.ds(0, MB), :] = mix_one[:, :PAIR]
            offset[pair, pl.ds(MB, MB), :] = mix_two[:, :PAIR] + through[:, :PAIR]
        return carry

    lax.fori_loop(0, groups, query_group, 0)

    own_half = (iota((HD, PAIR), 1) // HD) == lax.rem(me, 2)

    def state_copy(s):
        return pltpu.make_async_remote_copy(
            src_ref=sent_state.at[s], dst_ref=got_state.at[me],
            send_sem=state_send.at[s], recv_sem=state_recv.at[me],
            device_id={"seq": s}, device_id_type=MESH)

    def map_arrival(s):
        return pltpu.make_async_remote_copy(
            src_ref=sent_map.at[s], dst_ref=got_map.at[s],
            send_sem=map_send.at[s], recv_sem=map_recv.at[s],
            device_id={"seq": s}, device_id_type=MESH)

    def state_arrival(h):
        return pltpu.make_async_remote_copy(
            src_ref=sent_state.at[h], dst_ref=got_state.at[h],
            send_sem=state_send.at[h], recv_sem=state_recv.at[h],
            device_id={"seq": h}, device_id_type=MESH)

    def chain(s, state):
        message = jnp.where(own_half, state, 0.0).astype(BF16)
        sent_state[s] = message

        @pl.when(s == me)
        def _():
            got_state[me] = message

        @pl.when(s != me)
        def _():
            state_copy(s).start()
            map_arrival(s).wait_recv()

        step = got_map[s]
        wide_step = step.astype(F32)
        offsets = jnp.where(lane_low, wide_step, pltpu.roll(wide_step, HD, 1))
        operand = jnp.concatenate([jnp.zeros((HD, PAIR), BF16), state.astype(BF16)], axis=0)
        return state - dot(step, operand) + offsets

    start = jnp.concatenate([init_v[...], init_v[...]], axis=1)
    lax.fori_loop(0, seq_count, chain, start)

    for pair in range(heads // 2):
        for h in (2 * pair, 2 * pair + 1):
            @pl.when(h != me)
            def _():
                state_arrival(h).wait_recv()
        state = jnp.concatenate([got_state[2 * pair], got_state[2 * pair + 1]], axis=0)
        inner[:, pair * PAIR:(pair + 1) * PAIR] = (
            dot(query_map[pair], state) + offset[pair]).astype(BF16)

    for n in range(chunks):
        out_weight_copy(n).wait()
        piece = slice(n * chunk, (n + 1) * chunk)
        result[:, piece] = (
            hidden[:, piece].astype(F32) + dot(inner[...], wout_v[n])).astype(BF16)

        @pl.when(section == 0)
        def _():
            hidden_copy(n).start()

        result_copy(n).start()

    for n in range(chunks):
        result_copy(n).wait()

    @pl.when(section == 0)
    def _():
        for n in range(chunks):
            hidden_copy(n).wait_send()

    def drain(s, carry):
        @pl.when(s != me)
        def _():
            map_copy(s).wait_send()
            state_copy(s).wait_send()
        return carry

    lax.fori_loop(0, seq_count, drain, 0)


def solution(mesh):
    seq_count = mesh.shape["seq"]

    def shards(tokens, norm_gain, w_qkv, w_rate, rate_base, init_state, w_out):
        rows, width = tokens.shape
        heads = rate_base.shape[1]
        inner_width = heads * HD
        groups = inner_width // GROUP
        chunks = 4
        chunk = width // chunks
        hbm = pl.BlockSpec(memory_space=pltpu.HBM)

        def body(*refs):
            kernel(seq_count, *refs)

        return pl.pallas_call(
            body,
            name="layers",
            out_shape=jax.ShapeDtypeStruct((1, rows, width), BF16),
            in_specs=[hbm] * 7,
            out_specs=hbm,
            scratch_shapes=[
                pltpu.VMEM((rows, width), BF16),
                pltpu.VMEM((1, width), F32),
                pltpu.VMEM((groups, width, 2 * GROUP), BF16),
                pltpu.VMEM((groups, width, GROUP), BF16),
                pltpu.VMEM((heads, width), BF16),
                pltpu.VMEM((1, heads), F32),
                pltpu.VMEM((chunks, inner_width, chunk), BF16),
                pltpu.VMEM((HD, HD), F32),
                pltpu.VMEM((rows, width), BF16),
                pltpu.VMEM((2, rows, heads), BF16),
                pltpu.VMEM((heads // 2, rows, PAIR), BF16),
                pltpu.VMEM((heads // 2, rows, 2 * PAIR), BF16),
                pltpu.VMEM((heads // 2, PAIR, 2 * PAIR), BF16),
                pltpu.VMEM((heads, HD, PAIR), BF16),
                pltpu.VMEM((seq_count, HD, PAIR), BF16),
                pltpu.VMEM((seq_count, HD, PAIR), BF16),
                pltpu.VMEM((heads, HD, PAIR), BF16),
                pltpu.VMEM((heads // 2, rows, PAIR), BF16),
                pltpu.VMEM((heads // 2, rows, PAIR), F32),
                pltpu.VMEM((rows, inner_width), BF16),
                pltpu.VMEM((rows, width), BF16),
                pltpu.SemaphoreType.DMA((5,)),
                pltpu.SemaphoreType.DMA((4, max(groups, chunks))),
                pltpu.SemaphoreType.DMA((chunks,)),
                pltpu.SemaphoreType.DMA((heads,)),
                pltpu.SemaphoreType.DMA((seq_count,)),
                pltpu.SemaphoreType.DMA((seq_count,)),
                pltpu.SemaphoreType.DMA((heads,)),
                pltpu.SemaphoreType.DMA((chunks,)),
                pltpu.SemaphoreType.DMA((chunks,)),
            ],
            compiler_params=pltpu.CompilerParams(
                collective_id=0, has_side_effects=True, vmem_limit_bytes=63 * 1024 * 1024),
        )(tokens, norm_gain, w_qkv, jnp.swapaxes(w_rate, 1, 2), rate_base, init_state, w_out)

    return jax.shard_map(
        shards,
        mesh=mesh,
        in_specs=(
            P(("traj", "seq"), None),
            P("section", None),
            P("section", None, None),
            P("section", None, None),
            P("section", None),
            P("section", None, None, None),
            P("section", None, None),
        ),
        out_specs=P("section", ("traj", "seq"), None),
        check_vma=False,
    )
```

time: 648 us -> 51.1 us (0.08)
  the two profiles are of different devices: /device:TPU:8 before, /device:TPU:1 now
where the time goes in v1:
time: 51.1 us; the launch traced here: 51 us
  Pallas kernels  49.1 us (96%)
  local copies, waits for them, and re-layouts  1.88 us (4%)
    pallas_call x1, Pallas kernels, shards(): pl.pallas_call(body, name='layers', out_shape=jax.ShapeDtypeStruct((1, ro...  49.1 us
    unnamed x1, local copies, waits for them, and re-layouts  1.88 us

profile of v1, /device:TPU:1, one launch (start us, length us, event | category | flops | bytes accessed | tf_op | source)
XLA Modules:
  0.0 51.0 jit_solution(2081252677109961165)
XLA Ops:
  0.0 49.1 %layers.1 = bf16[1,128,2048]{2,1,0:T(8,128)(2,1)} custom-call(bf16[128,2048]{1,0:T(8,128)(2,1)} %refs_0_.1, f32[1,2048]{1,0:T(1,128)} %refs_1_.1, bf16[1,2048,3072]{2,1,0:T(8,128)(2,1)} %refs_2_.1, bf16[1,16,2048]{2,1,0:T(8,128)(2,1)} %bitcast.1, f32[1,16]{1,0:T(1,128)} %refs_4_.1, f32[1,16,64,64]{3,2,1,0:T(8,128)} %refs_5_.1, bf16[1,1024,2048]{2,1,0:T(8,128)(2,1)} %refs_6_.1), custom_call_target="tpu_custom_call" | custom-call | tf_op jit(solution)/shard_map/layers/pallas_call | solution.py:321
  49.1 1.9 %copy.9 = bf16[1,128,2048]{2,1,0:T(8,128)(2,1)} copy(bf16[1,128,2048]{2,1,0:T(8,128)(2,1)} %layers.1) | data formatting | bytes 1048576

commit v2 on v1

v2 whole, which is shorter than its diff:
```python
import jax
import jax.numpy as jnp
from jax import lax
from jax.experimental import pallas as pl
from jax.experimental.pallas import tpu as pltpu
from jax.sharding import PartitionSpec as P

HD = 64
MB = 64
PAIR = 2 * HD
GROUP = 4 * HD
EPS = 1e-06
MESH = pl.DeviceIdType.MESH
F32 = jnp.float32
BF16 = jnp.bfloat16


def dot(a, b, dims=((1,), (0,))):
    return lax.dot_general(a, b, (dims, ((), ())), preferred_element_type=F32)


def split(x):
    high = x.astype(BF16)
    return high, (x - high.astype(F32)).astype(BF16)


def iota(shape, axis):
    return lax.broadcasted_iota(jnp.int32, shape, axis)


def head_ones():
    same = iota((GROUP, GROUP), 0) // HD == iota((GROUP, GROUP), 1) // HD
    return jnp.where(same, 1.0, 0.0).astype(BF16)


def unit_scale(x, ones):
    return lax.rsqrt(dot((x * x).astype(BF16), ones) + EPS)


def kernel(
    seq_count,
    tok, gain, w_qkv, w_rate, rate_base, init_state, w_out,
    out,
    hidden, gain_v, wkv_v, wq_v, wrate_v, rbase_v, wout_v, init_v,
    normed, rate_all, keys, scaled, first_map, sent_map, got_map, sent_state, got_state,
    query_map, offset, result,
    load_sem, weight_sem, out_sem,
    map_send, map_recv, state_send, state_recv, hid_send, hid_recv,
):
    section = lax.axis_index("section")
    me = lax.axis_index("seq")
    rows, width = tok.shape
    heads = rate_base.shape[1]
    inner_width = heads * HD
    groups = inner_width // GROUP
    chunks = hid_send.shape[0]
    chunk = width // chunks

    token_copy = pltpu.make_async_copy(tok, hidden, load_sem.at[0])

    @pl.when(section == 0)
    def _():
        token_copy.start()

    small = [
        pltpu.make_async_copy(gain, gain_v, load_sem.at[1]),
        pltpu.make_async_copy(w_rate.at[0], wrate_v, load_sem.at[2]),
        pltpu.make_async_copy(rate_base, rbase_v, load_sem.at[3]),
        pltpu.make_async_copy(init_state.at[0, me], init_v, load_sem.at[4]),
    ]
    for copy in small:
        copy.start()

    def key_copy(g):
        return pltpu.make_async_copy(
            w_qkv.at[0, :, pl.ds(inner_width + g * GROUP, GROUP)],
            wkv_v.at[g, :, pl.ds(0, GROUP)], weight_sem.at[0, g])

    def value_copy(g):
        return pltpu.make_async_copy(
            w_qkv.at[0, :, pl.ds(2 * inner_width + g * GROUP, GROUP)],
            wkv_v.at[g, :, pl.ds(GROUP, GROUP)], weight_sem.at[1, g])

    def query_copy(g):
        return pltpu.make_async_copy(
            w_qkv.at[0, :, pl.ds(g * GROUP, GROUP)], wq_v.at[g], weight_sem.at[2, g])

    def out_weight_copy(n):
        return pltpu.make_async_copy(
            w_out.at[0, :, pl.ds(n * chunk, chunk)], wout_v.at[n], weight_sem.at[3, n])

    for g in range(groups):
        key_copy(g).start()
        value_copy(g).start()

    barrier = pltpu.get_barrier_semaphore()
    peers = [lax.rem(me + step, seq_count) for step in range(1, seq_count)]
    for peer in peers:
        pl.semaphore_signal(barrier, inc=1, device_id={"seq": peer}, device_id_type=MESH)
    pl.semaphore_signal(barrier, inc=1, device_id={"section": 1 - section}, device_id_type=MESH)

    def hidden_copy(n):
        piece = pl.ds(n * chunk, chunk)
        return pltpu.make_async_remote_copy(
            src_ref=result.at[:, piece], dst_ref=hidden.at[:, piece],
            send_sem=hid_send.at[n], recv_sem=hid_recv.at[n],
            device_id={"section": 1 - section}, device_id_type=MESH)

    def result_copy(n):
        piece = pl.ds(n * chunk, chunk)
        return pltpu.make_async_copy(result.at[:, piece], out.at[0, :, piece], out_sem.at[n])

    for copy in small:
        copy.wait()

    @pl.when(section == 0)
    def _():
        token_copy.wait()

    @pl.when(section == 1)
    def _():
        for n in range(chunks):
            hidden_copy(n).wait_recv()

    wide = hidden[...].astype(F32)
    mean_sq = jnp.mean(wide * wide, axis=-1, keepdims=True)
    normed[...] = (wide * lax.rsqrt(mean_sq + EPS) * gain_v[...]).astype(BF16)
    rates = rbase_v[...] * jax.nn.sigmoid(dot(normed[...], wrate_v[...], ((1,), (1,))))
    spread = jnp.where(
        iota((heads, inner_width), 0) == iota((heads, inner_width), 1) // HD, 1.0, 0.0).astype(BF16)
    high, low = split(rates)
    rate_all[...] = dot(high, spread) + dot(low, spread)

    lane_low = iota((HD, PAIR), 1) < HD
    wide_shape = (PAIR, 4 * PAIR)
    diagonal = iota(wide_shape, 0) // HD == (iota(wide_shape, 1) % PAIR) // HD
    ones = head_ones()
    blank = jnp.zeros((MB, 2 * PAIR), BF16)

    def map_copy(peer):
        return pltpu.make_async_remote_copy(
            src_ref=sent_map.at[peer], dst_ref=got_map.at[me],
            send_sem=map_send.at[peer], recv_sem=map_recv.at[me],
            device_id={"seq": peer}, device_id_type=MESH)

    def key_group(g):
        both = dot(normed[...], wkv_v[g])
        key, value = both[:, :GROUP], both[:, GROUP:]
        scale = unit_scale(key, ones)
        rate = rate_all[:, g * GROUP:(g + 1) * GROUP] * scale
        key_bf = key.astype(BF16)
        rated_value = (rate * value).astype(BF16)
        rated_key = (rate * scale * key).astype(BF16)
        for i in range(2):
            lanes = slice(i * PAIR, (i + 1) * PAIR)
            pair = 2 * g + i
            pair_key = key_bf[:, lanes]
            pair_scaled = jnp.concatenate([rated_value[:, lanes], rated_key[:, lanes]], axis=1)
            keys[pair] = pair_key
            scaled[pair] = pair_scaled
            by_block = jnp.concatenate([
                jnp.concatenate([pair_scaled[:MB], blank], axis=1),
                jnp.concatenate([blank, pair_scaled[MB:]], axis=1)], axis=0)
            maps = jnp.where(diagonal, dot(pair_key, by_block, ((0,), (0,))), 0.0)
            first, second = maps[:, :2 * PAIR], maps[:, 2 * PAIR:]
            first_bf = first.astype(BF16)
            first_map[pair] = first_bf
            total = first + second - dot(second[:, PAIR:].astype(BF16), first_bf)
            packed = total[:HD] + total[HD:]
            pack_b, pack_d = packed[:, :PAIR], pltpu.roll(packed[:, PAIR:], HD, 1)
            sent_map[2 * pair] = jnp.where(lane_low, pack_b, pack_d).astype(BF16)
            sent_map[2 * pair + 1] = jnp.where(lane_low, pack_d, pack_b).astype(BF16)

    half = groups // 2
    for g in range(half):
        key_copy(g).wait()
        value_copy(g).wait()
    for g in range(groups):
        query_copy(g).start()
    for g in range(half):
        key_group(g)
    for g in range(half, groups):
        key_copy(g).wait()
        value_copy(g).wait()
    for n in range(chunks):
        out_weight_copy(n).start()
    for g in range(half, groups):
        key_group(g)

    pl.semaphore_wait(barrier, seq_count)
    for peer in peers:
        map_copy(peer).start()
    got_map[me] = sent_map[me]

    row = iota((4 * MB, PAIR), 0)
    column = iota((4 * MB, PAIR), 1)
    causal = (column // MB == row // PAIR) & (column % MB <= row % MB)
    low_half = iota((MB, 2 * PAIR), 1) % PAIR < HD

    def query_group(g):
        query_all = dot(normed[...], wq_v[g])
        scale_all = unit_scale(query_all, ones)
        for i in range(2):
            pair = 2 * g + i
            query = query_all[:, i * PAIR:(i + 1) * PAIR]
            scale = scale_all[:, i * PAIR:(i + 1) * PAIR]
            parts = []
            for b in range(2):
                piece = query[b * MB:(b + 1) * MB]
                parts += [jnp.where(lane_low, piece, 0.0), jnp.where(lane_low, 0.0, piece)]
            stacked = jnp.concatenate(parts, axis=0).astype(BF16)
            scores = jnp.where(causal, dot(stacked, keys[pair], ((1,), (1,))), 0.0).astype(BF16)
            mixed = dot(scores, scaled[pair])
            mix_one = jnp.where(low_half, mixed[:MB], mixed[MB:2 * MB])
            mix_two = jnp.where(low_half, mixed[2 * MB:3 * MB], mixed[3 * MB:])
            map_one = query[:MB] - mix_one[:, PAIR:]
            map_two = query[MB:] - mix_two[:, PAIR:]
            through = dot(map_two.astype(BF16), first_map[pair])
            query_map[pair, pl.ds(0, MB), :] = (scale[:MB] * map_one).astype(BF16)
            query_map[pair, pl.ds(MB, MB), :] = (
                scale[MB:] * (map_two - through[:, PAIR:])).astype(BF16)
            offset[pair, pl.ds(0, MB), :] = scale[:MB] * mix_one[:, :PAIR]
            offset[pair, pl.ds(MB, MB), :] = (
                scale[MB:] * (mix_two[:, :PAIR] + through[:, :PAIR]))

    for g in range(groups):
        query_copy(g).wait()
    for g in range(half):
        query_group(g)

    odd = lax.rem(me, 2)
    offset_half = (iota((HD, PAIR), 1) // HD) == odd

    def state_copy(peer):
        return pltpu.make_async_remote_copy(
            src_ref=sent_state.at[peer], dst_ref=got_state.at[me],
            send_sem=state_send.at[peer], recv_sem=state_recv.at[me],
            device_id={"seq": peer}, device_id_type=MESH)

    def map_arrival(peer):
        return pltpu.make_async_remote_copy(
            src_ref=sent_map.at[peer], dst_ref=got_map.at[peer],
            send_sem=map_send.at[peer], recv_sem=map_recv.at[peer],
            device_id={"seq": peer}, device_id_type=MESH)

    def state_arrival(peer):
        return pltpu.make_async_remote_copy(
            src_ref=sent_state.at[peer], dst_ref=got_state.at[peer],
            send_sem=state_send.at[peer], recv_sem=state_recv.at[peer],
            device_id={"seq": peer}, device_id_type=MESH)

    for peer in peers:
        map_arrival(peer).wait_recv()

    def after(later, earlier):
        contracted = jnp.where(offset_half, 0.0, later).astype(BF16)
        operand = earlier.astype(BF16)
        return earlier + later - dot(contracted, jnp.concatenate([operand, operand], axis=0))

    step = [got_map[s].astype(F32) for s in range(seq_count)]
    state = [None] * seq_count
    state[0] = jnp.where(offset_half, jnp.concatenate([init_v[...], init_v[...]], axis=1), 0.0)
    prefix = {}
    for g in range(seq_count // 4):
        lead = 4 * g
        prefix[g, 1] = step[lead]
        prefix[g, 2] = after(step[lead + 1], step[lead])
        if g + 1 < seq_count // 4:
            prefix[g, 4] = after(after(step[lead + 3], step[lead + 2]), prefix[g, 2])
        prefix[g, 3] = after(step[lead + 2], prefix[g, 2])
    state[4] = after(prefix[0, 4], state[0])
    state[8] = after(after(prefix[1, 4], prefix[0, 4]), state[0])
    state[12] = after(after(prefix[2, 4], prefix[1, 4]), state[4])
    for g in range(seq_count // 4):
        for i in range(1, 4):
            state[4 * g + i] = after(prefix[g, i], state[4 * g])
    for s in range(seq_count):
        sent_state[s] = jnp.where(offset_half, state[s], 0.0).astype(BF16)
    for peer in peers:
        state_copy(peer).start()
    got_state[me] = sent_state[me]

    for g in range(half, groups):
        query_group(g)

    for n in range(chunks):
        out_weight_copy(n).wait()
    for peer in peers:
        state_arrival(peer).wait_recv()
    parts = []
    for pair in range(heads // 2):
        start = jnp.concatenate([got_state[2 * pair], got_state[2 * pair + 1]], axis=0)
        parts.append((dot(query_map[pair], start) + offset[pair]).astype(BF16))
    inner = jnp.concatenate(parts, axis=1)

    for n in range(chunks):
        piece = slice(n * chunk, (n + 1) * chunk)
        result[:, piece] = (hidden[:, piece].astype(F32) + dot(inner, wout_v[n])).astype(BF16)

        @pl.when(section == 0)
        def _():
            hidden_copy(n).start()

        result_copy(n).start()

    for peer in peers:
        map_copy(peer).wait_send()
        state_copy(peer).wait_send()
    for n in range(chunks):
        result_copy(n).wait()

    @pl.when(section == 0)
    def _():
        for n in range(chunks):
            hidden_copy(n).wait_send()


def solution(mesh):
    seq_count = mesh.shape["seq"]

    def shards(tokens, norm_gain, w_qkv, w_rate, rate_base, init_state, w_out):
        rows, width = tokens.shape
        heads = rate_base.shape[1]
        inner_width = heads * HD
        groups = inner_width // GROUP
        chunks = 4
        chunk = width // chunks
        hbm = pl.BlockSpec(memory_space=pltpu.HBM)

        def body(*refs):
            kernel(seq_count, *refs)

        return pl.pallas_call(
            body,
            name="layers",
            out_shape=jax.ShapeDtypeStruct((1, rows, width), BF16),
            in_specs=[hbm] * 7,
            out_specs=hbm,
            scratch_shapes=[
                pltpu.VMEM((rows, width), BF16),
                pltpu.VMEM((1, width), F32),
                pltpu.VMEM((groups, width, 2 * GROUP), BF16),
                pltpu.VMEM((groups, width, GROUP), BF16),
                pltpu.VMEM((heads, width), BF16),
                pltpu.VMEM((1, heads), F32),
                pltpu.VMEM((chunks, inner_width, chunk), BF16),
                pltpu.VMEM((HD, HD), F32),
                pltpu.VMEM((rows, width), BF16),
                pltpu.VMEM((rows, inner_width), F32),
                pltpu.VMEM((heads // 2, rows, PAIR), BF16),
                pltpu.VMEM((heads // 2, rows, 2 * PAIR), BF16),
                pltpu.VMEM((heads // 2, PAIR, 2 * PAIR), BF16),
                pltpu.VMEM((heads, HD, PAIR), BF16),
                pltpu.VMEM((seq_count, HD, PAIR), BF16),
                pltpu.VMEM((seq_count, HD, PAIR), BF16),
                pltpu.VMEM((heads, HD, PAIR), BF16),
                pltpu.VMEM((heads // 2, rows, PAIR), BF16),
                pltpu.VMEM((heads // 2, rows, PAIR), F32),
                pltpu.VMEM((rows, width), BF16),
                pltpu.SemaphoreType.DMA((5,)),
                pltpu.SemaphoreType.DMA((4, max(groups, chunks))),
                pltpu.SemaphoreType.DMA((chunks,)),
                pltpu.SemaphoreType.DMA((heads,)),
                pltpu.SemaphoreType.DMA((seq_count,)),
                pltpu.SemaphoreType.DMA((seq_count,)),
                pltpu.SemaphoreType.DMA((heads,)),
                pltpu.SemaphoreType.DMA((chunks,)),
                pltpu.SemaphoreType.DMA((chunks,)),
            ],
            compiler_params=pltpu.CompilerParams(
                collective_id=0, has_side_effects=True, vmem_limit_bytes=63 * 1024 * 1024),
        )(tokens, norm_gain, w_qkv, jnp.swapaxes(w_rate, 1, 2), rate_base, init_state, w_out)

    return jax.shard_map(
        shards,
        mesh=mesh,
        in_specs=(
            P(("traj", "seq"), None),
            P("section", None),
            P("section", None, None),
            P("section", None, None),
            P("section", None),
            P("section", None, None, None),
            P("section", None, None),
        ),
        out_specs=P("section", ("traj", "seq"), None),
        check_vma=False,
    )
```

time: 51.1 us -> 45.2 us (0.88)
  Pallas kernels: 49.1 us -> 43.2 us
    pallas_call x1, Pallas kernels: 49.1 us -> 43.2 us  [shards(): pl.pallas_call(body, name='layers', out_shape=jax.ShapeDtypeStruct((1, ro...]
where the time goes in v2:
time: 45.2 us; the launch traced here: 45.1 us
  Pallas kernels  43.2 us (96%)
  local copies, waits for them, and re-layouts  1.88 us (4%)
    pallas_call x1, Pallas kernels, shards(): pl.pallas_call(body, name='layers', out_shape=jax.ShapeDtypeStruct((1, ro...  43.2 us
    unnamed x1, local copies, waits for them, and re-layouts  1.88 us

profile of v2, /device:TPU:1, one launch (start us, length us, event | category | flops | bytes accessed | tf_op | source)
XLA Modules:
  0.0 45.1 jit_solution(4208038097696915098)
XLA Ops:
  0.0 43.2 %layers.1 = bf16[1,128,2048]{2,1,0:T(8,128)(2,1)} custom-call(bf16[128,2048]{1,0:T(8,128)(2,1)} %refs_0_.1, f32[1,2048]{1,0:T(1,128)} %refs_1_.1, bf16[1,2048,3072]{2,1,0:T(8,128)(2,1)} %refs_2_.1, bf16[1,16,2048]{2,1,0:T(8,128)(2,1)} %bitcast.1, f32[1,16]{1,0:T(1,128)} %refs_4_.1, f32[1,16,64,64]{3,2,1,0:T(8,128)} %refs_5_.1, bf16[1,1024,2048]{2,1,0:T(8,128)(2,1)} %refs_6_.1), custom_call_target="tpu_custom_call" | custom-call | tf_op jit(solution)/shard_map/layers/pallas_call | solution.py:333
  43.2 1.9 %copy.9 = bf16[1,128,2048]{2,1,0:T(8,128)(2,1)} copy(bf16[1,128,2048]{2,1,0:T(8,128)(2,1)} %layers.1) | data formatting | bytes 1048576

commit v3 on v2

--- a/solution.py
+++ b/solution.py
@@ -43,8 +43,8 @@
     out,
     hidden, gain_v, wkv_v, wq_v, wrate_v, rbase_v, wout_v, init_v,
     normed, rate_all, keys, scaled, first_map, sent_map, got_map, sent_state, got_state,
-    query_map, offset, result,
-    load_sem, weight_sem, out_sem,
+    query_map, offset,
+    load_sem, weight_sem,
     map_send, map_recv, state_send, state_recv, hid_send, hid_recv,
 ):
     section = lax.axis_index("section")
@@ -94,7 +94,13 @@
         value_copy(g).start()
 
     barrier = pltpu.get_barrier_semaphore()
-    peers = [lax.rem(me + step, seq_count) for step in range(1, seq_count)]
+    side = 4
+    row_of, column_of = me // side, lax.rem(me, side)
+    steps = [(y, x) for y in range(seq_count // side) for x in range(side)][1:]
+    steps.sort(key=lambda s: -min(s[0], seq_count // side - s[0]) - min(s[1], side - s[1]))
+    peers = [
+        lax.rem(row_of + y, seq_count // side) * side + lax.rem(column_of + x, side)
+        for y, x in steps]
     for peer in peers:
         pl.semaphore_signal(barrier, inc=1, device_id={"seq": peer}, device_id_type=MESH)
     pl.semaphore_signal(barrier, inc=1, device_id={"section": 1 - section}, device_id_type=MESH)
@@ -102,13 +108,9 @@
     def hidden_copy(n):
         piece = pl.ds(n * chunk, chunk)
         return pltpu.make_async_remote_copy(
-            src_ref=result.at[:, piece], dst_ref=hidden.at[:, piece],
+            src_ref=out.at[0, :, piece], dst_ref=hidden.at[:, piece],
             send_sem=hid_send.at[n], recv_sem=hid_recv.at[n],
             device_id={"section": 1 - section}, device_id_type=MESH)
-
-    def result_copy(n):
-        piece = pl.ds(n * chunk, chunk)
-        return pltpu.make_async_copy(result.at[:, piece], out.at[0, :, piece], out_sem.at[n])
 
     for copy in small:
         copy.wait()
@@ -179,6 +181,12 @@
         query_copy(g).start()
     for g in range(half):
         key_group(g)
+    pl.semaphore_wait(barrier, seq_count)
+    for h in range(heads // 2):
+        @pl.when(h != me)
+        def _():
+            map_copy(h).start()
+
     for g in range(half, groups):
         key_copy(g).wait()
         value_copy(g).wait()
@@ -187,9 +195,11 @@
     for g in range(half, groups):
         key_group(g)
 
-    pl.semaphore_wait(barrier, seq_count)
-    for peer in peers:
-        map_copy(peer).start()
+    for h in range(heads // 2, heads):
+        @pl.when(h != me)
+        def _():
+            map_copy(h).start()
+
     got_map[me] = sent_map[me]
 
     row = iota((4 * MB, PAIR), 0)
@@ -295,19 +305,16 @@
 
     for n in range(chunks):
         piece = slice(n * chunk, (n + 1) * chunk)
-        result[:, piece] = (hidden[:, piece].astype(F32) + dot(inner, wout_v[n])).astype(BF16)
+        out[0, :, piece] = (hidden[:, piece].astype(F32) + dot(inner, wout_v[n])).astype(BF16)
 
         @pl.when(section == 0)
         def _():
             hidden_copy(n).start()
 
-        result_copy(n).start()
 
     for peer in peers:
         map_copy(peer).wait_send()
         state_copy(peer).wait_send()
-    for n in range(chunks):
-        result_copy(n).wait()
 
     @pl.when(section == 0)
     def _():
@@ -335,7 +342,7 @@
             name="layers",
             out_shape=jax.ShapeDtypeStruct((1, rows, width), BF16),
             in_specs=[hbm] * 7,
-            out_specs=hbm,
+            out_specs=pl.BlockSpec(memory_space=pltpu.VMEM),
             scratch_shapes=[
                 pltpu.VMEM((rows, width), BF16),
                 pltpu.VMEM((1, width), F32),
@@ -356,10 +363,8 @@
                 pltpu.VMEM((heads, HD, PAIR), BF16),
                 pltpu.VMEM((heads // 2, rows, PAIR), BF16),
                 pltpu.VMEM((heads // 2, rows, PAIR), F32),
-                pltpu.VMEM((rows, width), BF16),
                 pltpu.SemaphoreType.DMA((5,)),
                 pltpu.SemaphoreType.DMA((4, max(groups, chunks))),
-                pltpu.SemaphoreType.DMA((chunks,)),
                 pltpu.SemaphoreType.DMA((heads,)),
                 pltpu.SemaphoreType.DMA((seq_count,)),
                 pltpu.SemaphoreType.DMA((seq_count,)),
@@ -368,8 +373,12 @@
                 pltpu.SemaphoreType.DMA((chunks,)),
             ],
             compiler_params=pltpu.CompilerParams(
-                collective_id=0, has_side_effects=True, vmem_limit_bytes=63 * 1024 * 1024),
-        )(tokens, norm_gain, w_qkv, jnp.swapaxes(w_rate, 1, 2), rate_base, init_state, w_out)
+                collective_id=0, has_side_effects=True, vmem_limit_bytes=40 * 1024 * 1024),
+        )(*(
+            pltpu.with_memory_space_constraint(array, pltpu.HBM)
+            for array in (
+                tokens, norm_gain, w_qkv, jnp.swapaxes(w_rate, 1, 2), rate_base, init_state, w_out)
+        ))
 
     return jax.shard_map(
         shards,

time: 45.2 us -> 42.4 us (0.938)
  Pallas kernels: 43.2 us -> 41.5 us
  local copies, waits for them, and re-layouts: 1.88 us -> 0.8 us
    pallas_call x1, Pallas kernels: 43.2 us -> 41.5 us  [shards(): pl.pallas_call(body, name='layers', out_shape=jax.ShapeDtypeStruct((1, ro...]
    unnamed x1, local copies, waits for them, and re-layouts: 1.88 us -> 0.8 us
where the time goes in v3:
time: 42.4 us; the launch traced here: 42.3 us
  Pallas kernels  41.5 us (98%)
  local copies, waits for them, and re-layouts  0.8 us (2%)
    pallas_call x1, Pallas kernels, shards(): pl.pallas_call(body, name='layers', out_shape=jax.ShapeDtypeStruct((1, ro...  41.5 us

profile of v3, /device:TPU:1, one launch (start us, length us, event | category | flops | bytes accessed | tf_op | source)
XLA Modules:
  0.0 42.3 jit_solution(3650390161774354863)
XLA Ops:
  0.0 41.5 %layers.1 = bf16[1,128,2048]{2,1,0:T(8,128)(2,1)S(1)} custom-call(bf16[128,2048]{1,0:T(8,128)(2,1)} %refs_0_.1, f32[1,2048]{1,0:T(1,128)} %refs_1_.1, bf16[1,2048,3072]{2,1,0:T(8,128)(2,1)} %refs_2_.1, bf16[1,16,2048]{2,1,0:T(8,128)(2,1)} %bitcast.1, f32[1,16]{1,0:T(1,128)} %refs_4_.1, f32[1,16,64,64]{3,2,1,0:T(8,128)} %refs_5_.1, bf16[1,1024,2048]{2,1,0:T(8,128)(2,1)} %refs_6_.1), custom_call_target="tpu_custom_call" | custom-call | tf_op jit(solution)/shard_map/layers/pallas_call | solution.py:340
  41.5 0.8 %copy.9 = bf16[1,128,2048]{2,1,0:T(8,128)(2,1)} copy(bf16[1,128,2048]{2,1,0:T(8,128)(2,1)S(1)} %layers.1) | data formatting | bytes 1048576

commit v4 on v3

--- a/solution.py
+++ b/solution.py
@@ -33,8 +33,8 @@
     return jnp.where(same, 1.0, 0.0).astype(BF16)
 
 
-def unit_scale(x, ones):
-    return lax.rsqrt(dot((x * x).astype(BF16), ones) + EPS)
+def unit_scale(x, row_scale, ones):
+    return row_scale * lax.rsqrt(row_scale * row_scale * dot((x * x).astype(BF16), ones) + EPS)
 
 
 def kernel(
@@ -42,10 +42,10 @@
     tok, gain, w_qkv, w_rate, rate_base, init_state, w_out,
     out,
     hidden, gain_v, wkv_v, wq_v, wrate_v, rbase_v, wout_v, init_v,
-    normed, rate_all, keys, scaled, first_map, sent_map, got_map, sent_state, got_state,
-    query_map, offset,
+    normed, scaled_rows, rate_all, keys, scaled, first_map, sent_map, got_map, sent_state, got_state,
+    query_map, offset, wout_first, state_first, query_first, offset_first,
     load_sem, weight_sem,
-    map_send, map_recv, state_send, state_recv, hid_send, hid_recv,
+    map_send, map_recv, state_send, state_recv, first_send, first_recv, side_send, side_recv,
 ):
     section = lax.axis_index("section")
     me = lax.axis_index("seq")
@@ -53,15 +53,11 @@
     heads = rate_base.shape[1]
     inner_width = heads * HD
     groups = inner_width // GROUP
-    chunks = hid_send.shape[0]
+    chunks = wout_v.shape[0]
     chunk = width // chunks
 
     token_copy = pltpu.make_async_copy(tok, hidden, load_sem.at[0])
-
-    @pl.when(section == 0)
-    def _():
-        token_copy.start()
-
+    token_copy.start()
     small = [
         pltpu.make_async_copy(gain, gain_v, load_sem.at[1]),
         pltpu.make_async_copy(w_rate.at[0], wrate_v, load_sem.at[2]),
@@ -89,7 +85,8 @@
         return pltpu.make_async_copy(
             w_out.at[0, :, pl.ds(n * chunk, chunk)], wout_v.at[n], weight_sem.at[3, n])
 
-    for g in range(groups):
+    half = groups // 2
+    for g in range(half):
         key_copy(g).start()
         value_copy(g).start()
 
@@ -102,32 +99,80 @@
         lax.rem(row_of + y, seq_count // side) * side + lax.rem(column_of + x, side)
         for y, x in steps]
     for peer in peers:
-        pl.semaphore_signal(barrier, inc=1, device_id={"seq": peer}, device_id_type=MESH)
+        for other in range(2):
+            pl.semaphore_signal(
+                barrier, inc=1, device_id={"section": other, "seq": peer}, device_id_type=MESH)
     pl.semaphore_signal(barrier, inc=1, device_id={"section": 1 - section}, device_id_type=MESH)
-
-    def hidden_copy(n):
-        piece = pl.ds(n * chunk, chunk)
-        return pltpu.make_async_remote_copy(
-            src_ref=out.at[0, :, piece], dst_ref=hidden.at[:, piece],
-            send_sem=hid_send.at[n], recv_sem=hid_recv.at[n],
+    entered = 2 * seq_count - 1
+
+    def tail(maps, offsets, states, weights, write):
+        parts = []
+        for pair in range(heads // 2):
+            start = jnp.concatenate([states[2 * pair], states[2 * pair + 1]], axis=0)
+            parts.append((dot(maps[pair], start) + offsets[pair]).astype(BF16))
+        inner = jnp.concatenate(parts, axis=1)
+        for n in range(chunks):
+            piece = slice(n * chunk, (n + 1) * chunk)
+            write(piece, (hidden[:, piece].astype(F32) + dot(inner, weights[n])).astype(BF16))
+
+    half_pairs = heads // 4
+
+    def side_copy(index):
+        if index < chunks:
+            source, target = wout_v.at[index], wout_first.at[index]
+        else:
+            pairs = pl.ds((index - chunks) // 2 * half_pairs, half_pairs)
+            source, target = [
+                (query_map.at[pairs], query_first.at[pairs]),
+                (offset.at[pairs], offset_first.at[pairs])][(index - chunks) % 2]
+        return pltpu.make_async_remote_copy(
+            src_ref=source, dst_ref=target,
+            send_sem=side_send.at[index], recv_sem=side_recv.at[index],
             device_id={"section": 1 - section}, device_id_type=MESH)
+
+    def first_copy(peer):
+        return pltpu.make_async_remote_copy(
+            src_ref=sent_state.at[peer], dst_ref=state_first.at[me],
+            send_sem=first_send.at[peer], recv_sem=first_recv.at[me],
+            device_id={"section": 1 - section, "seq": peer}, device_id_type=MESH)
+
+    def first_arrival(peer):
+        return pltpu.make_async_remote_copy(
+            src_ref=sent_state.at[peer], dst_ref=state_first.at[peer],
+            send_sem=first_send.at[peer], recv_sem=first_recv.at[peer],
+            device_id={"section": 1 - section, "seq": peer}, device_id_type=MESH)
 
     for copy in small:
         copy.wait()
-
-    @pl.when(section == 0)
-    def _():
-        token_copy.wait()
+    token_copy.wait()
 
     @pl.when(section == 1)
     def _():
-        for n in range(chunks):
-            hidden_copy(n).wait_recv()
-
+        for index in range(chunks + 4):
+            side_copy(index).wait_recv()
+        for peer in peers + [me]:
+            first_arrival(peer).wait_recv()
+
+        def write(piece, value):
+            hidden[:, piece] = value
+
+        tail(query_first, offset_first, state_first, wout_first, write)
+
+    for g in range(1):
+        key_copy(g).wait()
+        value_copy(g).wait()
+    for g in range(half, groups):
+        key_copy(g).start()
+        value_copy(g).start()
+    for g in range(1, half):
+        key_copy(g).wait()
+        value_copy(g).wait()
     wide = hidden[...].astype(F32)
-    mean_sq = jnp.mean(wide * wide, axis=-1, keepdims=True)
-    normed[...] = (wide * lax.rsqrt(mean_sq + EPS) * gain_v[...]).astype(BF16)
-    rates = rbase_v[...] * jax.nn.sigmoid(dot(normed[...], wrate_v[...], ((1,), (1,))))
+    row_scale = lax.rsqrt(jnp.mean(wide * wide, axis=-1, keepdims=True) + EPS)
+    scaled_rows[...] = jnp.broadcast_to(row_scale, (rows, PAIR))
+    normed[...] = (wide * gain_v[...]).astype(BF16)
+    rates = rbase_v[...] * jax.nn.sigmoid(
+        row_scale * dot(normed[...], wrate_v[...], ((1,), (1,))))
     spread = jnp.where(
         iota((heads, inner_width), 0) == iota((heads, inner_width), 1) // HD, 1.0, 0.0).astype(BF16)
     high, low = split(rates)
@@ -145,13 +190,17 @@
             send_sem=map_send.at[peer], recv_sem=map_recv.at[me],
             device_id={"seq": peer}, device_id_type=MESH)
 
+    def row_factor():
+        return jnp.concatenate([scaled_rows[...]] * (GROUP // PAIR), axis=1)
+
     def key_group(g):
         both = dot(normed[...], wkv_v[g])
         key, value = both[:, :GROUP], both[:, GROUP:]
-        scale = unit_scale(key, ones)
+        row_wide = row_factor()
+        scale = unit_scale(key, row_wide, ones)
         rate = rate_all[:, g * GROUP:(g + 1) * GROUP] * scale
         key_bf = key.astype(BF16)
-        rated_value = (rate * value).astype(BF16)
+        rated_value = (rate * (row_wide * value)).astype(BF16)
         rated_key = (rate * scale * key).astype(BF16)
         for i in range(2):
             lanes = slice(i * PAIR, (i + 1) * PAIR)
@@ -173,23 +222,19 @@
             sent_map[2 * pair] = jnp.where(lane_low, pack_b, pack_d).astype(BF16)
             sent_map[2 * pair + 1] = jnp.where(lane_low, pack_d, pack_b).astype(BF16)
 
-    half = groups // 2
     for g in range(half):
+        key_group(g)
+    pl.semaphore_wait(barrier, entered)
+    for h in range(heads // 2):
+        @pl.when(h != me)
+        def _():
+            map_copy(h).start()
+
+    for g in range(half, groups):
         key_copy(g).wait()
         value_copy(g).wait()
     for g in range(groups):
         query_copy(g).start()
-    for g in range(half):
-        key_group(g)
-    pl.semaphore_wait(barrier, seq_count)
-    for h in range(heads // 2):
-        @pl.when(h != me)
-        def _():
-            map_copy(h).start()
-
-    for g in range(half, groups):
-        key_copy(g).wait()
-        value_copy(g).wait()
     for n in range(chunks):
         out_weight_copy(n).start()
     for g in range(half, groups):
@@ -209,7 +254,7 @@
 
     def query_group(g):
         query_all = dot(normed[...], wq_v[g])
-        scale_all = unit_scale(query_all, ones)
+        scale_all = unit_scale(query_all, row_factor(), ones)
         for i in range(2):
             pair = 2 * g + i
             query = query_all[:, i * PAIR:(i + 1) * PAIR]
@@ -235,8 +280,30 @@
 
     for g in range(groups):
         query_copy(g).wait()
+    for n in range(chunks):
+        out_weight_copy(n).wait()
+
+    @pl.when(section == 0)
+    def _():
+        for n in range(chunks):
+            side_copy(n).start()
+
     for g in range(half):
         query_group(g)
+
+    @pl.when(section == 0)
+    def _():
+        for index in range(chunks, chunks + 2):
+            side_copy(index).start()
+
+
+    for g in range(half, groups):
+        query_group(g)
+
+    @pl.when(section == 0)
+    def _():
+        for index in range(chunks + 2, chunks + 4):
+            side_copy(index).start()
 
     odd = lax.rem(me, 2)
     offset_half = (iota((HD, PAIR), 1) // HD) == odd
@@ -286,31 +353,23 @@
             state[4 * g + i] = after(prefix[g, i], state[4 * g])
     for s in range(seq_count):
         sent_state[s] = jnp.where(offset_half, state[s], 0.0).astype(BF16)
+
+    @pl.when(section == 0)
+    def _():
+        for peer in peers + [me]:
+            first_copy(peer).start()
+
     for peer in peers:
         state_copy(peer).start()
     got_state[me] = sent_state[me]
 
-    for g in range(half, groups):
-        query_group(g)
-
-    for n in range(chunks):
-        out_weight_copy(n).wait()
     for peer in peers:
         state_arrival(peer).wait_recv()
-    parts = []
-    for pair in range(heads // 2):
-        start = jnp.concatenate([got_state[2 * pair], got_state[2 * pair + 1]], axis=0)
-        parts.append((dot(query_map[pair], start) + offset[pair]).astype(BF16))
-    inner = jnp.concatenate(parts, axis=1)
-
-    for n in range(chunks):
-        piece = slice(n * chunk, (n + 1) * chunk)
-        out[0, :, piece] = (hidden[:, piece].astype(F32) + dot(inner, wout_v[n])).astype(BF16)
-
-        @pl.when(section == 0)
-        def _():
-            hidden_copy(n).start()
-
+
+    def write_out(piece, value):
+        out[0, :, piece] = value
+
+    tail(query_map, offset, got_state, wout_v, write_out)
 
     for peer in peers:
         map_copy(peer).wait_send()
@@ -318,8 +377,10 @@
 
     @pl.when(section == 0)
     def _():
-        for n in range(chunks):
-            hidden_copy(n).wait_send()
+        for index in range(chunks + 4):
+            side_copy(index).wait_send()
+        for peer in peers + [me]:
+            first_copy(peer).wait_send()
 
 
 def solution(mesh):
@@ -353,6 +414,7 @@
                 pltpu.VMEM((chunks, inner_width, chunk), BF16),
                 pltpu.VMEM((HD, HD), F32),
                 pltpu.VMEM((rows, width), BF16),
+                pltpu.VMEM((rows, PAIR), F32),
                 pltpu.VMEM((rows, inner_width), F32),
                 pltpu.VMEM((heads // 2, rows, PAIR), BF16),
                 pltpu.VMEM((heads // 2, rows, 2 * PAIR), BF16),
@@ -363,14 +425,20 @@
                 pltpu.VMEM((heads, HD, PAIR), BF16),
                 pltpu.VMEM((heads // 2, rows, PAIR), BF16),
                 pltpu.VMEM((heads // 2, rows, PAIR), F32),
+                pltpu.VMEM((chunks, inner_width, chunk), BF16),
+                pltpu.VMEM((seq_count, HD, PAIR), BF16),
+                pltpu.VMEM((heads // 2, rows, PAIR), BF16),
+                pltpu.VMEM((heads // 2, rows, PAIR), F32),
                 pltpu.SemaphoreType.DMA((5,)),
                 pltpu.SemaphoreType.DMA((4, max(groups, chunks))),
                 pltpu.SemaphoreType.DMA((heads,)),
                 pltpu.SemaphoreType.DMA((seq_count,)),
                 pltpu.SemaphoreType.DMA((seq_count,)),
                 pltpu.SemaphoreType.DMA((heads,)),
-                pltpu.SemaphoreType.DMA((chunks,)),
-                pltpu.SemaphoreType.DMA((chunks,)),
+                pltpu.SemaphoreType.DMA((seq_count,)),
+                pltpu.SemaphoreType.DMA((seq_count,)),
+                pltpu.SemaphoreType.DMA((chunks + 4,)),
+                pltpu.SemaphoreType.DMA((chunks + 4,)),
             ],
             compiler_params=pltpu.CompilerParams(
                 collective_id=0, has_side_effects=True, vmem_limit_bytes=40 * 1024 * 1024),

time: 42.4 us -> 41.4 us (0.976)
  Pallas kernels: 41.5 us -> 40.6 us
    pallas_call x1, Pallas kernels: 41.5 us -> 40.6 us  [shards(): pl.pallas_call(body, name='layers', out_shape=jax.ShapeDtypeStruct((1, ro...]
where the time goes in v4:
time: 41.4 us
  Pallas kernels  40.6 us (98%)
  local copies, waits for them, and re-layouts  0.8 us (2%)
    pallas_call x1, Pallas kernels, shards(): pl.pallas_call(body, name='layers', out_shape=jax.ShapeDtypeStruct((1, ro...  40.6 us

profile of v4, /device:TPU:1, one launch (start us, length us, event | category | flops | bytes accessed | tf_op | source)
XLA Modules:
  0.0 41.4 jit_solution(8457744582028720055)
XLA Ops:
  0.0 40.6 %layers.1 = bf16[1,128,2048]{2,1,0:T(8,128)(2,1)S(1)} custom-call(bf16[128,2048]{1,0:T(8,128)(2,1)} %refs_0_.1, f32[1,2048]{1,0:T(1,128)} %refs_1_.1, bf16[1,2048,3072]{2,1,0:T(8,128)(2,1)} %refs_2_.1, bf16[1,16,2048]{2,1,0:T(8,128)(2,1)} %bitcast.1, f32[1,16]{1,0:T(1,128)} %refs_4_.1, f32[1,16,64,64]{3,2,1,0:T(8,128)} %refs_5_.1, bf16[1,1024,2048]{2,1,0:T(8,128)(2,1)} %refs_6_.1), custom_call_target="tpu_custom_call" | custom-call | tf_op jit(solution)/shard_map/layers/pallas_call | solution.py:401
  40.6 0.8 %copy.9 = bf16[1,128,2048]{2,1,0:T(8,128)(2,1)} copy(bf16[1,128,2048]{2,1,0:T(8,128)(2,1)S(1)} %layers.1) | data formatting | bytes 1048576

commit v5 on v4

--- a/solution.py
+++ b/solution.py
@@ -148,6 +148,21 @@
 
     @pl.when(section == 1)
     def _():
+        for g in range(half, groups):
+            key_copy(g).start()
+            value_copy(g).start()
+        for g in range(groups):
+            query_copy(g).start()
+        for n in range(chunks):
+            out_weight_copy(n).start()
+        for g in range(groups):
+            key_copy(g).wait()
+            value_copy(g).wait()
+        for g in range(groups):
+            query_copy(g).wait()
+        for n in range(chunks):
+            out_weight_copy(n).wait()
+        pl.semaphore_wait(barrier, entered)
         for index in range(chunks + 4):
             side_copy(index).wait_recv()
         for peer in peers + [me]:
@@ -158,15 +173,17 @@
 
         tail(query_first, offset_first, state_first, wout_first, write)
 
-    for g in range(1):
-        key_copy(g).wait()
-        value_copy(g).wait()
-    for g in range(half, groups):
-        key_copy(g).start()
-        value_copy(g).start()
-    for g in range(1, half):
-        key_copy(g).wait()
-        value_copy(g).wait()
+    @pl.when(section == 0)
+    def _():
+        key_copy(0).wait()
+        value_copy(0).wait()
+        for g in range(half, groups):
+            key_copy(g).start()
+            value_copy(g).start()
+        for g in range(1, half):
+            key_copy(g).wait()
+            value_copy(g).wait()
+
     wide = hidden[...].astype(F32)
     row_scale = lax.rsqrt(jnp.mean(wide * wide, axis=-1, keepdims=True) + EPS)
     scaled_rows[...] = jnp.broadcast_to(row_scale, (rows, PAIR))
@@ -222,28 +239,36 @@
             sent_map[2 * pair] = jnp.where(lane_low, pack_b, pack_d).astype(BF16)
             sent_map[2 * pair + 1] = jnp.where(lane_low, pack_d, pack_b).astype(BF16)
 
-    for g in range(half):
-        key_group(g)
-    pl.semaphore_wait(barrier, entered)
-    for h in range(heads // 2):
-        @pl.when(h != me)
-        def _():
-            map_copy(h).start()
-
-    for g in range(half, groups):
-        key_copy(g).wait()
-        value_copy(g).wait()
-    for g in range(groups):
-        query_copy(g).start()
-    for n in range(chunks):
-        out_weight_copy(n).start()
-    for g in range(half, groups):
-        key_group(g)
-
-    for h in range(heads // 2, heads):
-        @pl.when(h != me)
-        def _():
-            map_copy(h).start()
+    @pl.when(section == 0)
+    def _():
+        for g in range(half):
+            key_group(g)
+        for g in range(groups):
+            query_copy(g).start()
+        pl.semaphore_wait(barrier, entered)
+        for h in range(heads // 2):
+            @pl.when(h != me)
+            def _():
+                map_copy(h).start()
+
+        for g in range(half, groups):
+            key_copy(g).wait()
+            value_copy(g).wait()
+        for n in range(chunks):
+            out_weight_copy(n).start()
+        for g in range(half, groups):
+            key_group(g)
+        for h in range(heads // 2, heads):
+            @pl.when(h != me)
+            def _():
+                map_copy(h).start()
+
+    @pl.when(section == 1)
+    def _():
+        for g in range(groups):
+            key_group(g)
+        for peer in peers:
+            map_copy(peer).start()
 
     got_map[me] = sent_map[me]
 
@@ -278,24 +303,20 @@
             offset[pair, pl.ds(MB, MB), :] = (
                 scale[MB:] * (mix_two[:, :PAIR] + through[:, :PAIR]))
 
-    for g in range(groups):
-        query_copy(g).wait()
-    for n in range(chunks):
-        out_weight_copy(n).wait()
-
-    @pl.when(section == 0)
-    def _():
-        for n in range(chunks):
-            side_copy(n).start()
+    @pl.when(section == 0)
+    def _():
+        for g in range(groups):
+            query_copy(g).wait()
 
     for g in range(half):
         query_group(g)
 
     @pl.when(section == 0)
     def _():
-        for index in range(chunks, chunks + 2):
+        for n in range(chunks):
+            out_weight_copy(n).wait()
+        for index in range(chunks + 2):
             side_copy(index).start()
-
 
     for g in range(half, groups):
         query_group(g)

time: 41.4 us -> 39 us (0.942)
  Pallas kernels: 40.6 us -> 38.1 us
    pallas_call x1, Pallas kernels: 40.6 us -> 38.1 us  [shards(): pl.pallas_call(body, name='layers', out_shape=jax.ShapeDtypeStruct((1, ro...]
where the time goes in v5:
time: 39 us; the launch traced here: 38.9 us
  Pallas kernels  38.1 us (98%)
  local copies, waits for them, and re-layouts  0.8 us (2%)
    pallas_call x1, Pallas kernels, shards(): pl.pallas_call(body, name='layers', out_shape=jax.ShapeDtypeStruct((1, ro...  38.1 us
    unnamed x1, local copies, waits for them, and re-layouts  0.8 us

profile of v5, /device:TPU:1, one launch (start us, length us, event | category | flops | bytes accessed | tf_op | source)
XLA Modules:
  0.0 38.9 jit_solution(13844441062959869069)
XLA Ops:
  0.0 38.1 %layers.1 = bf16[1,128,2048]{2,1,0:T(8,128)(2,1)S(1)} custom-call(bf16[128,2048]{1,0:T(8,128)(2,1)} %refs_0_.1, f32[1,2048]{1,0:T(1,128)} %refs_1_.1, bf16[1,2048,3072]{2,1,0:T(8,128)(2,1)} %refs_2_.1, bf16[1,16,2048]{2,1,0:T(8,128)(2,1)} %bitcast.1, f32[1,16]{1,0:T(1,128)} %refs_4_.1, f32[1,16,64,64]{3,2,1,0:T(8,128)} %refs_5_.1, bf16[1,1024,2048]{2,1,0:T(8,128)(2,1)} %refs_6_.1), custom_call_target="tpu_custom_call" | custom-call | tf_op jit(solution)/shard_map/layers/pallas_call | solution.py:422
  38.1 0.8 %copy.9 = bf16[1,128,2048]{2,1,0:T(8,128)(2,1)} copy(bf16[1,128,2048]{2,1,0:T(8,128)(2,1)S(1)} %layers.1) | data formatting | bytes 1048576

commit v6 on v4

--- a/solution.py
+++ b/solution.py
@@ -146,37 +146,22 @@
         copy.wait()
     token_copy.wait()
 
-    @pl.when(section == 1)
-    def _():
-        for index in range(chunks + 4):
-            side_copy(index).wait_recv()
-        for peer in peers + [me]:
-            first_arrival(peer).wait_recv()
-
-        def write(piece, value):
-            hidden[:, piece] = value
-
-        tail(query_first, offset_first, state_first, wout_first, write)
-
-    for g in range(1):
-        key_copy(g).wait()
-        value_copy(g).wait()
-    for g in range(half, groups):
-        key_copy(g).start()
-        value_copy(g).start()
-    for g in range(1, half):
-        key_copy(g).wait()
-        value_copy(g).wait()
-    wide = hidden[...].astype(F32)
-    row_scale = lax.rsqrt(jnp.mean(wide * wide, axis=-1, keepdims=True) + EPS)
-    scaled_rows[...] = jnp.broadcast_to(row_scale, (rows, PAIR))
-    normed[...] = (wide * gain_v[...]).astype(BF16)
-    rates = rbase_v[...] * jax.nn.sigmoid(
-        row_scale * dot(normed[...], wrate_v[...], ((1,), (1,))))
-    spread = jnp.where(
-        iota((heads, inner_width), 0) == iota((heads, inner_width), 1) // HD, 1.0, 0.0).astype(BF16)
-    high, low = split(rates)
-    rate_all[...] = dot(high, spread) + dot(low, spread)
+    def norm():
+        wide = hidden[...].astype(F32)
+        row_scale = lax.rsqrt(jnp.mean(wide * wide, axis=-1, keepdims=True) + EPS)
+        scaled_rows[...] = jnp.broadcast_to(row_scale, (rows, PAIR))
+        normed[...] = (wide * gain_v[...]).astype(BF16)
+        return row_scale
+
+    def rate_parts(row_scale):
+        return split(rbase_v[...] * jax.nn.sigmoid(
+            row_scale * dot(normed[...], wrate_v[...], ((1,), (1,)))))
+
+    def rate_spread(parts):
+        spread = jnp.where(
+            iota((heads, inner_width), 0) == iota((heads, inner_width), 1) // HD,
+            1.0, 0.0).astype(BF16)
+        rate_all[...] = dot(parts[0], spread) + dot(parts[1], spread)
 
     lane_low = iota((HD, PAIR), 1) < HD
     wide_shape = (PAIR, 4 * PAIR)
@@ -193,8 +178,10 @@
     def row_factor():
         return jnp.concatenate([scaled_rows[...]] * (GROUP // PAIR), axis=1)
 
-    def key_group(g):
-        both = dot(normed[...], wkv_v[g])
+    def key_dot(g):
+        return dot(normed[...], wkv_v[g])
+
+    def key_scale(g, both):
         key, value = both[:, :GROUP], both[:, GROUP:]
         row_wide = row_factor()
         scale = unit_scale(key, row_wide, ones)
@@ -202,48 +189,122 @@
         key_bf = key.astype(BF16)
         rated_value = (rate * (row_wide * value)).astype(BF16)
         rated_key = (rate * scale * key).astype(BF16)
+        made = []
         for i in range(2):
             lanes = slice(i * PAIR, (i + 1) * PAIR)
-            pair = 2 * g + i
             pair_key = key_bf[:, lanes]
             pair_scaled = jnp.concatenate([rated_value[:, lanes], rated_key[:, lanes]], axis=1)
-            keys[pair] = pair_key
-            scaled[pair] = pair_scaled
+            keys[2 * g + i] = pair_key
+            scaled[2 * g + i] = pair_scaled
+            made.append((pair_key, pair_scaled))
+        return made
+
+    def key_maps(g, made):
+        found = []
+        for i, (pair_key, pair_scaled) in enumerate(made):
             by_block = jnp.concatenate([
                 jnp.concatenate([pair_scaled[:MB], blank], axis=1),
                 jnp.concatenate([blank, pair_scaled[MB:]], axis=1)], axis=0)
             maps = jnp.where(diagonal, dot(pair_key, by_block, ((0,), (0,))), 0.0)
+            first_bf = maps[:, :2 * PAIR].astype(BF16)
+            first_map[2 * g + i] = first_bf
+            found.append((maps, first_bf))
+        return found
+
+    def key_pack(g, found):
+        for i, (maps, first_bf) in enumerate(found):
+            pair = 2 * g + i
             first, second = maps[:, :2 * PAIR], maps[:, 2 * PAIR:]
-            first_bf = first.astype(BF16)
-            first_map[pair] = first_bf
             total = first + second - dot(second[:, PAIR:].astype(BF16), first_bf)
             packed = total[:HD] + total[HD:]
             pack_b, pack_d = packed[:, :PAIR], pltpu.roll(packed[:, PAIR:], HD, 1)
             sent_map[2 * pair] = jnp.where(lane_low, pack_b, pack_d).astype(BF16)
             sent_map[2 * pair + 1] = jnp.where(lane_low, pack_d, pack_b).astype(BF16)
 
-    for g in range(half):
-        key_group(g)
-    pl.semaphore_wait(barrier, entered)
-    for h in range(heads // 2):
-        @pl.when(h != me)
-        def _():
-            map_copy(h).start()
-
-    for g in range(half, groups):
-        key_copy(g).wait()
-        value_copy(g).wait()
-    for g in range(groups):
-        query_copy(g).start()
-    for n in range(chunks):
-        out_weight_copy(n).start()
-    for g in range(half, groups):
-        key_group(g)
-
-    for h in range(heads // 2, heads):
-        @pl.when(h != me)
-        def _():
-            map_copy(h).start()
+    def key_groups(which, before=lambda position: None, gap=0):
+        stages = [lambda g, unused: key_dot(g)]
+        stages += [lambda g, value: value] * gap + [key_scale, key_maps, key_pack]
+        held = {}
+        for step in range(len(which) + len(stages) - 1):
+            if step < len(which):
+                before(step)
+            for depth, stage in enumerate(stages):
+                position = step - depth
+                if 0 <= position < len(which):
+                    held[position] = stage(which[position], held.get(position))
+
+    @pl.when(section == 0)
+    def _():
+        for g in range(half, groups - 1):
+            key_copy(g).start()
+            value_copy(g).start()
+        rate_spread(rate_parts(norm()))
+        for g in range(half):
+            key_copy(g).wait()
+            value_copy(g).wait()
+            if g == 0:
+                key_copy(groups - 1).start()
+                value_copy(groups - 1).start()
+        key_groups(range(half))
+        for g in range(groups):
+            query_copy(g).start()
+        pl.semaphore_wait(barrier, entered)
+        for h in range(heads // 2):
+            @pl.when(h != me)
+            def _():
+                map_copy(h).start()
+
+        def arrive(position):
+            key_copy(half + position).wait()
+            value_copy(half + position).wait()
+            if position == groups - half - 1:
+                for n in range(chunks):
+                    out_weight_copy(n).start()
+
+        key_groups(range(half, groups), arrive)
+        for h in range(heads // 2, heads):
+            @pl.when(h != me)
+            def _():
+                map_copy(h).start()
+
+    @pl.when(section == 1)
+    def _():
+        for g in range(half, groups):
+            key_copy(g).start()
+            value_copy(g).start()
+        for g in range(groups):
+            query_copy(g).start()
+        for n in range(chunks):
+            out_weight_copy(n).start()
+        for g in range(groups):
+            key_copy(g).wait()
+            value_copy(g).wait()
+        for g in range(groups):
+            query_copy(g).wait()
+        for n in range(chunks):
+            out_weight_copy(n).wait()
+        pl.semaphore_wait(barrier, entered)
+        for index in range(chunks + 4):
+            side_copy(index).wait_recv()
+        for peer in peers + [me]:
+            first_arrival(peer).wait_recv()
+
+        def write(piece, value):
+            hidden[:, piece] = value
+
+        tail(query_first, offset_first, state_first, wout_first, write)
+        row_scale = norm()
+        parts = []
+
+        def rates(position):
+            if position == 1:
+                parts.append(rate_parts(row_scale))
+            if position == 2:
+                rate_spread(parts[0])
+
+        key_groups(range(groups), rates, gap=1)
+        for peer in peers:
+            map_copy(peer).start()
 
     got_map[me] = sent_map[me]
 
@@ -278,24 +339,20 @@
             offset[pair, pl.ds(MB, MB), :] = (
                 scale[MB:] * (mix_two[:, :PAIR] + through[:, :PAIR]))
 
-    for g in range(groups):
-        query_copy(g).wait()
-    for n in range(chunks):
-        out_weight_copy(n).wait()
-
     @pl.when(section == 0)
     def _():
-        for n in range(chunks):
-            side_copy(n).start()
+        for g in range(groups):
+            query_copy(g).wait()
 
     for g in range(half):
         query_group(g)
 
     @pl.when(section == 0)
     def _():
-        for index in range(chunks, chunks + 2):
+        for n in range(chunks):
+            out_weight_copy(n).wait()
+        for index in range(chunks + 2):
             side_copy(index).start()
-
 
     for g in range(half, groups):
         query_group(g)
@@ -337,20 +394,26 @@
     step = [got_map[s].astype(F32) for s in range(seq_count)]
     state = [None] * seq_count
     state[0] = jnp.where(offset_half, jnp.concatenate([init_v[...], init_v[...]], axis=1), 0.0)
-    prefix = {}
-    for g in range(seq_count // 4):
-        lead = 4 * g
-        prefix[g, 1] = step[lead]
-        prefix[g, 2] = after(step[lead + 1], step[lead])
-        if g + 1 < seq_count // 4:
-            prefix[g, 4] = after(after(step[lead + 3], step[lead + 2]), prefix[g, 2])
-        prefix[g, 3] = after(step[lead + 2], prefix[g, 2])
-    state[4] = after(prefix[0, 4], state[0])
-    state[8] = after(after(prefix[1, 4], prefix[0, 4]), state[0])
-    state[12] = after(after(prefix[2, 4], prefix[1, 4]), state[4])
-    for g in range(seq_count // 4):
-        for i in range(1, 4):
-            state[4 * g + i] = after(prefix[g, i], state[4 * g])
+    runs = range(seq_count // 4)
+    one = [step[4 * g] for g in runs]
+    two = [after(step[4 * g + 1], step[4 * g]) for g in runs]
+    last_two = [after(step[4 * g + 3], step[4 * g + 2]) for g in runs[:-1]]
+    four = [after(last_two[g], two[g]) for g in runs[:-1]]
+    three = [after(step[4 * g + 2], two[g]) for g in runs]
+    state[4] = after(four[0], state[0])
+    eight = after(four[1], four[0])
+    next_eight = after(four[2], four[1])
+    prefixes = (one, two, three)
+
+    def fill(g):
+        for i in range(3):
+            state[4 * g + i + 1] = after(prefixes[i][g], state[4 * g])
+
+    fill(0)
+    state[8] = after(eight, state[0])
+    state[12] = after(next_eight, state[4])
+    for g in runs[1:]:
+        fill(g)
     for s in range(seq_count):
         sent_state[s] = jnp.where(offset_half, state[s], 0.0).astype(BF16)
 

time: 41.4 us -> 35.8 us (0.86)
  Pallas kernels: 40.6 us -> 34.9 us
    pallas_call x1, Pallas kernels: 40.6 us -> 34.9 us  [shards(): pl.pallas_call(body, name='layers', out_shape=jax.ShapeDtypeStruct((1, ro...]
where the time goes in v6:
time: 35.8 us; the launch traced here: 35.7 us
  Pallas kernels  34.9 us (97%)
  local copies, waits for them, and re-layouts  0.8 us (2%)
    pallas_call x1, Pallas kernels, shards(): pl.pallas_call(body, name='layers', out_shape=jax.ShapeDtypeStruct((1, ro...  34.9 us
    unnamed x1, local copies, waits for them, and re-layouts  0.8 us

profile of v6, /device:TPU:1, one launch (start us, length us, event | category | flops | bytes accessed | tf_op | source)
XLA Modules:
  0.0 35.7 jit_solution(18223303155671374848)
XLA Ops:
  0.0 34.9 %layers.1 = bf16[1,128,2048]{2,1,0:T(8,128)(2,1)S(1)} custom-call(bf16[128,2048]{1,0:T(8,128)(2,1)} %refs_0_.1, f32[1,2048]{1,0:T(1,128)} %refs_1_.1, bf16[1,2048,3072]{2,1,0:T(8,128)(2,1)} %refs_2_.1, bf16[1,16,2048]{2,1,0:T(8,128)(2,1)} %bitcast.1, f32[1,16]{1,0:T(1,128)} %refs_4_.1, f32[1,16,64,64]{3,2,1,0:T(8,128)} %refs_5_.1, bf16[1,1024,2048]{2,1,0:T(8,128)(2,1)} %refs_6_.1), custom_call_target="tpu_custom_call" | custom-call | tf_op jit(solution)/shard_map/layers/pallas_call | solution.py:464
  34.9 0.8 %copy.9 = bf16[1,128,2048]{2,1,0:T(8,128)(2,1)} copy(bf16[1,128,2048]{2,1,0:T(8,128)(2,1)S(1)} %layers.1) | data formatting | bytes 1048576

commit v7 on v6

--- a/solution.py
+++ b/solution.py
@@ -53,8 +53,11 @@
     heads = rate_base.shape[1]
     inner_width = heads * HD
     groups = inner_width // GROUP
-    chunks = wout_v.shape[0]
+    chunks = 4
     chunk = width // chunks
+    side = 4
+    row_of, column_of = me // side, lax.rem(me, side)
+    order = [lax.rem(row_of + turn, groups) for turn in (2, 1, 3, 0)]
 
     token_copy = pltpu.make_async_copy(tok, hidden, load_sem.at[0])
     token_copy.start()
@@ -67,23 +70,26 @@
     for copy in small:
         copy.start()
 
-    def key_copy(g):
+    def columns(start, p):
+        return pl.ds(pl.multiple_of(start + order[p] * GROUP, GROUP), GROUP)
+
+    def key_copy(p):
         return pltpu.make_async_copy(
-            w_qkv.at[0, :, pl.ds(inner_width + g * GROUP, GROUP)],
-            wkv_v.at[g, :, pl.ds(0, GROUP)], weight_sem.at[0, g])
-
-    def value_copy(g):
+            w_qkv.at[0, :, columns(inner_width, p)],
+            wkv_v.at[p, :, pl.ds(0, GROUP)], weight_sem.at[0, p])
+
+    def value_copy(p):
         return pltpu.make_async_copy(
-            w_qkv.at[0, :, pl.ds(2 * inner_width + g * GROUP, GROUP)],
-            wkv_v.at[g, :, pl.ds(GROUP, GROUP)], weight_sem.at[1, g])
-
-    def query_copy(g):
+            w_qkv.at[0, :, columns(2 * inner_width, p)],
+            wkv_v.at[p, :, pl.ds(GROUP, GROUP)], weight_sem.at[1, p])
+
+    def query_copy(p):
         return pltpu.make_async_copy(
-            w_qkv.at[0, :, pl.ds(g * GROUP, GROUP)], wq_v.at[g], weight_sem.at[2, g])
-
-    def out_weight_copy(n):
+            w_qkv.at[0, :, columns(0, p)], wq_v.at[p], weight_sem.at[2, p])
+
+    def out_weight_copy(p):
         return pltpu.make_async_copy(
-            w_out.at[0, :, pl.ds(n * chunk, chunk)], wout_v.at[n], weight_sem.at[3, n])
+            w_out.at[0, columns(0, p), :], wout_v.at[p], weight_sem.at[3, p])
 
     half = groups // 2
     for g in range(half):
@@ -91,8 +97,6 @@
         value_copy(g).start()
 
     barrier = pltpu.get_barrier_semaphore()
-    side = 4
-    row_of, column_of = me // side, lax.rem(me, side)
     steps = [(y, x) for y in range(seq_count // side) for x in range(side)][1:]
     steps.sort(key=lambda s: -min(s[0], seq_count // side - s[0]) - min(s[1], side - s[1]))
     peers = [
@@ -108,23 +112,25 @@
     def tail(maps, offsets, states, weights, write):
         parts = []
         for pair in range(heads // 2):
-            start = jnp.concatenate([states[2 * pair], states[2 * pair + 1]], axis=0)
+            h = 2 * (2 * order[pair // 2] + pair % 2)
+            start = jnp.concatenate([states[h], states[h + 1]], axis=0)
             parts.append((dot(maps[pair], start) + offsets[pair]).astype(BF16))
         inner = jnp.concatenate(parts, axis=1)
         for n in range(chunks):
             piece = slice(n * chunk, (n + 1) * chunk)
-            write(piece, (hidden[:, piece].astype(F32) + dot(inner, weights[n])).astype(BF16))
-
-    half_pairs = heads // 4
+            weight = jnp.concatenate([weights[p, :, piece] for p in range(groups)], axis=0)
+            write(piece, (hidden[:, piece].astype(F32) + dot(inner, weight)).astype(BF16))
+
+    early_pairs = heads // 2 - 2
 
     def side_copy(index):
-        if index < chunks:
+        if index < groups:
             source, target = wout_v.at[index], wout_first.at[index]
         else:
-            pairs = pl.ds((index - chunks) // 2 * half_pairs, half_pairs)
+            pairs = pl.ds(0, early_pairs) if index < groups + 2 else pl.ds(early_pairs, 2)
             source, target = [
                 (query_map.at[pairs], query_first.at[pairs]),
-                (offset.at[pairs], offset_first.at[pairs])][(index - chunks) % 2]
+                (offset.at[pairs], offset_first.at[pairs])][(index - groups) % 2]
         return pltpu.make_async_remote_copy(
             src_ref=source, dst_ref=target,
             send_sem=side_send.at[index], recv_sem=side_recv.at[index],
@@ -158,9 +164,9 @@
             row_scale * dot(normed[...], wrate_v[...], ((1,), (1,)))))
 
     def rate_spread(parts):
-        spread = jnp.where(
-            iota((heads, inner_width), 0) == iota((heads, inner_width), 1) // HD,
-            1.0, 0.0).astype(BF16)
+        head, lane = iota((heads, GROUP), 0), iota((heads, GROUP), 1)
+        spread = jnp.concatenate([
+            jnp.where(head == side * g + lane // HD, 1.0, 0.0) for g in order], axis=1).astype(BF16)
         rate_all[...] = dot(parts[0], spread) + dot(parts[1], spread)
 
     lane_low = iota((HD, PAIR), 1) < HD
@@ -213,17 +219,22 @@
 
     def key_pack(g, found):
         for i, (maps, first_bf) in enumerate(found):
-            pair = 2 * g + i
             first, second = maps[:, :2 * PAIR], maps[:, 2 * PAIR:]
             total = first + second - dot(second[:, PAIR:].astype(BF16), first_bf)
             packed = total[:HD] + total[HD:]
             pack_b, pack_d = packed[:, :PAIR], pltpu.roll(packed[:, PAIR:], HD, 1)
-            sent_map[2 * pair] = jnp.where(lane_low, pack_b, pack_d).astype(BF16)
-            sent_map[2 * pair + 1] = jnp.where(lane_low, pack_d, pack_b).astype(BF16)
+            h = side * order[g] + 2 * i
+            sent_map[h] = jnp.where(lane_low, pack_b, pack_d).astype(BF16)
+            sent_map[h + 1] = jnp.where(lane_low, pack_d, pack_b).astype(BF16)
+        own = g == groups - 1
+        for turn in (2, 1, 3) if own else (2, 1, 3, 0):
+            map_copy(side * order[g] + lax.rem(column_of + turn, side)).start()
 
     def key_groups(which, before=lambda position: None, gap=0):
-        stages = [lambda g, unused: key_dot(g)]
-        stages += [lambda g, value: value] * gap + [key_scale, key_maps, key_pack]
+        wait = [lambda g, value: value] * gap
+        pipeline([lambda g, unused: key_dot(g)] + wait + [key_scale, key_maps, key_pack], which, before)
+
+    def pipeline(stages, which, before=lambda position: None):
         held = {}
         for step in range(len(which) + len(stages) - 1):
             if step < len(which):
@@ -239,6 +250,7 @@
             key_copy(g).start()
             value_copy(g).start()
         rate_spread(rate_parts(norm()))
+        pl.semaphore_wait(barrier, entered)
         for g in range(half):
             key_copy(g).wait()
             value_copy(g).wait()
@@ -248,24 +260,14 @@
         key_groups(range(half))
         for g in range(groups):
             query_copy(g).start()
-        pl.semaphore_wait(barrier, entered)
-        for h in range(heads // 2):
-            @pl.when(h != me)
-            def _():
-                map_copy(h).start()
-
         def arrive(position):
             key_copy(half + position).wait()
             value_copy(half + position).wait()
             if position == groups - half - 1:
-                for n in range(chunks):
+                for n in range(groups):
                     out_weight_copy(n).start()
 
         key_groups(range(half, groups), arrive)
-        for h in range(heads // 2, heads):
-            @pl.when(h != me)
-            def _():
-                map_copy(h).start()
 
     @pl.when(section == 1)
     def _():
@@ -274,17 +276,17 @@
             value_copy(g).start()
         for g in range(groups):
             query_copy(g).start()
-        for n in range(chunks):
+        for n in range(groups):
             out_weight_copy(n).start()
         for g in range(groups):
             key_copy(g).wait()
             value_copy(g).wait()
         for g in range(groups):
             query_copy(g).wait()
-        for n in range(chunks):
+        for n in range(groups):
             out_weight_copy(n).wait()
         pl.semaphore_wait(barrier, entered)
-        for index in range(chunks + 4):
+        for index in range(groups + 4):
             side_copy(index).wait_recv()
         for peer in peers + [me]:
             first_arrival(peer).wait_recv()
@@ -303,8 +305,6 @@
                 rate_spread(parts[0])
 
         key_groups(range(groups), rates, gap=1)
-        for peer in peers:
-            map_copy(peer).start()
 
     got_map[me] = sent_map[me]
 
@@ -313,53 +313,59 @@
     causal = (column // MB == row // PAIR) & (column % MB <= row % MB)
     low_half = iota((MB, 2 * PAIR), 1) % PAIR < HD
 
-    def query_group(g):
-        query_all = dot(normed[...], wq_v[g])
+    def query_scores(g, query_all):
         scale_all = unit_scale(query_all, row_factor(), ones)
+        made = []
         for i in range(2):
-            pair = 2 * g + i
             query = query_all[:, i * PAIR:(i + 1) * PAIR]
-            scale = scale_all[:, i * PAIR:(i + 1) * PAIR]
             parts = []
             for b in range(2):
                 piece = query[b * MB:(b + 1) * MB]
                 parts += [jnp.where(lane_low, piece, 0.0), jnp.where(lane_low, 0.0, piece)]
             stacked = jnp.concatenate(parts, axis=0).astype(BF16)
-            scores = jnp.where(causal, dot(stacked, keys[pair], ((1,), (1,))), 0.0).astype(BF16)
+            scores = jnp.where(causal, dot(stacked, keys[2 * g + i], ((1,), (1,))), 0.0)
+            made.append((query, scale_all[:, i * PAIR:(i + 1) * PAIR], scores.astype(BF16)))
+        return made
+
+    def query_mix(g, made):
+        found = []
+        for i, (query, scale, scores) in enumerate(made):
+            pair = 2 * g + i
             mixed = dot(scores, scaled[pair])
             mix_one = jnp.where(low_half, mixed[:MB], mixed[MB:2 * MB])
             mix_two = jnp.where(low_half, mixed[2 * MB:3 * MB], mixed[3 * MB:])
             map_one = query[:MB] - mix_one[:, PAIR:]
             map_two = query[MB:] - mix_two[:, PAIR:]
+            query_map[pair, pl.ds(0, MB), :] = (scale[:MB] * map_one).astype(BF16)
+            offset[pair, pl.ds(0, MB), :] = scale[:MB] * mix_one[:, :PAIR]
+            found.append((map_two, mix_two[:, :PAIR], scale[MB:]))
+        return found
+
+    def query_through(g, found):
+        for i, (map_two, mix_two, scale) in enumerate(found):
+            pair = 2 * g + i
             through = dot(map_two.astype(BF16), first_map[pair])
-            query_map[pair, pl.ds(0, MB), :] = (scale[:MB] * map_one).astype(BF16)
             query_map[pair, pl.ds(MB, MB), :] = (
-                scale[MB:] * (map_two - through[:, PAIR:])).astype(BF16)
-            offset[pair, pl.ds(0, MB), :] = scale[:MB] * mix_one[:, :PAIR]
-            offset[pair, pl.ds(MB, MB), :] = (
-                scale[MB:] * (mix_two[:, :PAIR] + through[:, :PAIR]))
+                scale * (map_two - through[:, PAIR:])).astype(BF16)
+            offset[pair, pl.ds(MB, MB), :] = scale * (mix_two + through[:, :PAIR])
+
+    def query_groups(which):
+        pipeline(
+            [lambda g, unused: dot(normed[...], wq_v[g]), query_scores, query_mix, query_through],
+            which)
 
     @pl.when(section == 0)
     def _():
         for g in range(groups):
             query_copy(g).wait()
 
-    for g in range(half):
-        query_group(g)
+    query_groups(range(groups - 1))
 
     @pl.when(section == 0)
     def _():
-        for n in range(chunks):
+        for n in range(groups):
             out_weight_copy(n).wait()
-        for index in range(chunks + 2):
-            side_copy(index).start()
-
-    for g in range(half, groups):
-        query_group(g)
-
-    @pl.when(section == 0)
-    def _():
-        for index in range(chunks + 2, chunks + 4):
+        for index in range(groups + 2):
             side_copy(index).start()
 
     odd = lax.rem(me, 2)
@@ -426,6 +432,13 @@
         state_copy(peer).start()
     got_state[me] = sent_state[me]
 
+    query_groups(range(groups - 1, groups))
+
+    @pl.when(section == 0)
+    def _():
+        for index in range(groups + 2, groups + 4):
+            side_copy(index).start()
+
     for peer in peers:
         state_arrival(peer).wait_recv()
 
@@ -440,7 +453,7 @@
 
     @pl.when(section == 0)
     def _():
-        for index in range(chunks + 4):
+        for index in range(groups + 4):
             side_copy(index).wait_send()
         for peer in peers + [me]:
             first_copy(peer).wait_send()
@@ -454,8 +467,6 @@
         heads = rate_base.shape[1]
         inner_width = heads * HD
         groups = inner_width // GROUP
-        chunks = 4
-        chunk = width // chunks
         hbm = pl.BlockSpec(memory_space=pltpu.HBM)
 
         def body(*refs):
@@ -474,7 +485,7 @@
                 pltpu.VMEM((groups, width, GROUP), BF16),
                 pltpu.VMEM((heads, width), BF16),
                 pltpu.VMEM((1, heads), F32),
-                pltpu.VMEM((chunks, inner_width, chunk), BF16),
+                pltpu.VMEM((groups, GROUP, width), BF16),
                 pltpu.VMEM((HD, HD), F32),
                 pltpu.VMEM((rows, width), BF16),
                 pltpu.VMEM((rows, PAIR), F32),
@@ -488,20 +499,20 @@
                 pltpu.VMEM((heads, HD, PAIR), BF16),
                 pltpu.VMEM((heads // 2, rows, PAIR), BF16),
                 pltpu.VMEM((heads // 2, rows, PAIR), F32),
-                pltpu.VMEM((chunks, inner_width, chunk), BF16),
+                pltpu.VMEM((groups, GROUP, width), BF16),
                 pltpu.VMEM((seq_count, HD, PAIR), BF16),
                 pltpu.VMEM((heads // 2, rows, PAIR), BF16),
                 pltpu.VMEM((heads // 2, rows, PAIR), F32),
                 pltpu.SemaphoreType.DMA((5,)),
-                pltpu.SemaphoreType.DMA((4, max(groups, chunks))),
+                pltpu.SemaphoreType.DMA((4, groups)),
                 pltpu.SemaphoreType.DMA((heads,)),
                 pltpu.SemaphoreType.DMA((seq_count,)),
                 pltpu.SemaphoreType.DMA((seq_count,)),
                 pltpu.SemaphoreType.DMA((heads,)),
                 pltpu.SemaphoreType.DMA((seq_count,)),
                 pltpu.SemaphoreType.DMA((seq_count,)),
-                pltpu.SemaphoreType.DMA((chunks + 4,)),
-                pltpu.SemaphoreType.DMA((chunks + 4,)),
+                pltpu.SemaphoreType.DMA((groups + 4,)),
+                pltpu.SemaphoreType.DMA((groups + 4,)),
             ],
             compiler_params=pltpu.CompilerParams(
                 collective_id=0, has_side_effects=True, vmem_limit_bytes=40 * 1024 * 1024),

time: 35.8 us -> 34.9 us (0.975)
  Pallas kernels: 34.9 us -> 34 us
    pallas_call x1, Pallas kernels: 34.9 us -> 34 us  [shards(): pl.pallas_call(body, name='layers', out_shape=jax.ShapeDtypeStruct((1, ro...]
where the time goes in v7:
time: 34.9 us; the launch traced here: 34.8 us
  Pallas kernels  34 us (97%)
  local copies, waits for them, and re-layouts  0.8 us (2%)
    pallas_call x1, Pallas kernels, shards(): pl.pallas_call(body, name='layers', out_shape=jax.ShapeDtypeStruct((1, ro...  34 us
    unnamed x1, local copies, waits for them, and re-layouts  0.8 us

profile of v7, /device:TPU:1, one launch (start us, length us, event | category | flops | bytes accessed | tf_op | source)
XLA Modules:
  0.0 34.8 jit_solution(16765881138786901453)
XLA Ops:
  0.0 34.0 %layers.1 = bf16[1,128,2048]{2,1,0:T(8,128)(2,1)S(1)} custom-call(bf16[128,2048]{1,0:T(8,128)(2,1)} %refs_0_.1, f32[1,2048]{1,0:T(1,128)} %refs_1_.1, bf16[1,2048,3072]{2,1,0:T(8,128)(2,1)} %refs_2_.1, bf16[1,16,2048]{2,1,0:T(8,128)(2,1)} %bitcast.1, f32[1,16]{1,0:T(1,128)} %refs_4_.1, f32[1,16,64,64]{3,2,1,0:T(8,128)} %refs_5_.1, bf16[1,1024,2048]{2,1,0:T(8,128)(2,1)} %refs_6_.1), custom_call_target="tpu_custom_call" | custom-call | tf_op jit(solution)/shard_map/layers/pallas_call | solution.py:475
  34.0 0.8 %copy.9 = bf16[1,128,2048]{2,1,0:T(8,128)(2,1)} copy(bf16[1,128,2048]{2,1,0:T(8,128)(2,1)S(1)} %layers.1) | data formatting | bytes 1048576

commit v8 on v7

--- a/solution.py
+++ b/solution.py
@@ -109,11 +109,18 @@
     pl.semaphore_signal(barrier, inc=1, device_id={"section": 1 - section}, device_id_type=MESH)
     entered = 2 * seq_count - 1
 
+    def spread_state(packed, parity):
+        packed = packed.astype(F32)
+        own = (iota(packed.shape, 1) // HD) == parity
+        return [
+            jnp.where(own, part, 0.0).astype(BF16)
+            for part in (packed, pltpu.roll(packed, HD, 1))]
+
     def tail(maps, offsets, states, weights, write):
         parts = []
         for pair in range(heads // 2):
             h = 2 * (2 * order[pair // 2] + pair % 2)
-            start = jnp.concatenate([states[h], states[h + 1]], axis=0)
+            start = jnp.concatenate(spread_state(states[h], 0) + spread_state(states[h + 1], 1), axis=0)
             parts.append((dot(maps[pair], start) + offsets[pair]).astype(BF16))
         inner = jnp.concatenate(parts, axis=1)
         for n in range(chunks):
@@ -420,16 +427,22 @@
     state[12] = after(next_eight, state[4])
     for g in runs[1:]:
         fill(g)
+    own_half = (iota((HD // 2, PAIR), 1) // HD) == odd
     for s in range(seq_count):
-        sent_state[s] = jnp.where(offset_half, state[s], 0.0).astype(BF16)
+        sent_state[s] = jnp.where(
+            own_half, state[s][:HD // 2],
+            pltpu.roll(state[s][HD // 2:], HD, 1)).astype(BF16)
 
     @pl.when(section == 0)
     def _():
         for peer in peers + [me]:
             first_copy(peer).start()
 
-    for peer in peers:
-        state_copy(peer).start()
+    @pl.when(section == 1)
+    def _():
+        for peer in peers:
+            state_copy(peer).start()
+
     got_state[me] = sent_state[me]
 
     query_groups(range(groups - 1, groups))
@@ -438,6 +451,8 @@
     def _():
         for index in range(groups + 2, groups + 4):
             side_copy(index).start()
+        for peer in peers:
+            state_copy(peer).start()
 
     for peer in peers:
         state_arrival(peer).wait_recv()
@@ -495,12 +510,12 @@
                 pltpu.VMEM((heads // 2, PAIR, 2 * PAIR), BF16),
                 pltpu.VMEM((heads, HD, PAIR), BF16),
                 pltpu.VMEM((seq_count, HD, PAIR), BF16),
-                pltpu.VMEM((seq_count, HD, PAIR), BF16),
-                pltpu.VMEM((heads, HD, PAIR), BF16),
+                pltpu.VMEM((seq_count, HD // 2, PAIR), BF16),
+                pltpu.VMEM((heads, HD // 2, PAIR), BF16),
                 pltpu.VMEM((heads // 2, rows, PAIR), BF16),
                 pltpu.VMEM((heads // 2, rows, PAIR), F32),
                 pltpu.VMEM((groups, GROUP, width), BF16),
-                pltpu.VMEM((seq_count, HD, PAIR), BF16),
+                pltpu.VMEM((seq_count, HD // 2, PAIR), BF16),
                 pltpu.VMEM((heads // 2, rows, PAIR), BF16),
                 pltpu.VMEM((heads // 2, rows, PAIR), F32),
                 pltpu.SemaphoreType.DMA((5,)),

time: 34.9 us -> 34.8 us (level)
  no operation moved by 1% of the time
where the time goes in v8:
time: 34.8 us; the launch traced here: 34.7 us
  Pallas kernels  33.9 us (97%)
  local copies, waits for them, and re-layouts  0.8 us (2%)
    pallas_call x1, Pallas kernels, shards(): pl.pallas_call(body, name='layers', out_shape=jax.ShapeDtypeStruct((1, ro...  33.9 us
    unnamed x1, local copies, waits for them, and re-layouts  0.8 us

profile of v8, /device:TPU:1, one launch (start us, length us, event | category | flops | bytes accessed | tf_op | source)
XLA Modules:
  0.0 34.7 jit_solution(1663808553356447963)
XLA Ops:
  0.0 33.9 %layers.1 = bf16[1,128,2048]{2,1,0:T(8,128)(2,1)S(1)} custom-call(bf16[128,2048]{1,0:T(8,128)(2,1)} %refs_0_.1, f32[1,2048]{1,0:T(1,128)} %refs_1_.1, bf16[1,2048,3072]{2,1,0:T(8,128)(2,1)} %refs_2_.1, bf16[1,16,2048]{2,1,0:T(8,128)(2,1)} %bitcast.1, f32[1,16]{1,0:T(1,128)} %refs_4_.1, f32[1,16,64,64]{3,2,1,0:T(8,128)} %refs_5_.1, bf16[1,1024,2048]{2,1,0:T(8,128)(2,1)} %refs_6_.1), custom_call_target="tpu_custom_call" | custom-call | tf_op jit(solution)/shard_map/layers/pallas_call | solution.py:490
  33.9 0.8 %copy.9 = bf16[1,128,2048]{2,1,0:T(8,128)(2,1)} copy(bf16[1,128,2048]{2,1,0:T(8,128)(2,1)S(1)} %layers.1) | data formatting | bytes 1048576

commit v9 on v8

--- a/solution.py
+++ b/solution.py
@@ -455,16 +455,15 @@
             state_copy(peer).start()
 
     for peer in peers:
+        map_copy(peer).wait_send()
+        state_copy(peer).wait_send()
+    for peer in peers:
         state_arrival(peer).wait_recv()
 
     def write_out(piece, value):
         out[0, :, piece] = value
 
     tail(query_map, offset, got_state, wout_v, write_out)
-
-    for peer in peers:
-        map_copy(peer).wait_send()
-        state_copy(peer).wait_send()
 
     @pl.when(section == 0)
     def _():

time: 34.8 us -> 34.7 us (level)
  no operation moved by 1% of the time
where the time goes in v9:
time: 34.7 us; the launch traced here: 34.6 us
  Pallas kernels  33.8 us (97%)
  local copies, waits for them, and re-layouts  0.8 us (2%)
    pallas_call x1, Pallas kernels, shards(): pl.pallas_call(body, name='layers', out_shape=jax.ShapeDtypeStruct((1, ro...  33.8 us
    unnamed x1, local copies, waits for them, and re-layouts  0.8 us

profile of v9, /device:TPU:1, one launch (start us, length us, event | category | flops | bytes accessed | tf_op | source)
XLA Modules:
  0.0 34.6 jit_solution(5588756011537164835)
XLA Ops:
  0.0 33.8 %layers.1 = bf16[1,128,2048]{2,1,0:T(8,128)(2,1)S(1)} custom-call(bf16[128,2048]{1,0:T(8,128)(2,1)} %refs_0_.1, f32[1,2048]{1,0:T(1,128)} %refs_1_.1, bf16[1,2048,3072]{2,1,0:T(8,128)(2,1)} %refs_2_.1, bf16[1,16,2048]{2,1,0:T(8,128)(2,1)} %bitcast.1, f32[1,16]{1,0:T(1,128)} %refs_4_.1, f32[1,16,64,64]{3,2,1,0:T(8,128)} %refs_5_.1, bf16[1,1024,2048]{2,1,0:T(8,128)(2,1)} %refs_6_.1), custom_call_target="tpu_custom_call" | custom-call | tf_op jit(solution)/shard_map/layers/pallas_call | solution.py:489
  33.8 0.8 %copy.9 = bf16[1,128,2048]{2,1,0:T(8,128)(2,1)} copy(bf16[1,128,2048]{2,1,0:T(8,128)(2,1)S(1)} %layers.1) | data formatting | bytes 1048576

commit v10 on v9

--- a/solution.py
+++ b/solution.py
@@ -132,7 +132,7 @@
 
     def side_copy(index):
         if index < groups:
-            source, target = wout_v.at[index], wout_first.at[index]
+            source, target = w_out.at[0, columns(0, index), :], wout_first.at[index]
         else:
             pairs = pl.ds(0, early_pairs) if index < groups + 2 else pl.ds(early_pairs, 2)
             source, target = [
@@ -363,6 +363,8 @@
 
     @pl.when(section == 0)
     def _():
+        for index in range(groups):
+            side_copy(index).start()
         for g in range(groups):
             query_copy(g).wait()
 
@@ -372,7 +374,7 @@
     def _():
         for n in range(groups):
             out_weight_copy(n).wait()
-        for index in range(groups + 2):
+        for index in range(groups, groups + 2):
             side_copy(index).start()
 
     odd = lax.rem(me, 2)

time: 34.7 us -> 34.2 us (0.986)
  Pallas kernels: 33.8 us -> 33.3 us
    pallas_call x1, Pallas kernels: 33.8 us -> 33.3 us  [shards(): pl.pallas_call(body, name='layers', out_shape=jax.ShapeDtypeStruct((1, ro...]
where the time goes in v10:
time: 34.2 us; the launch traced here: 34.1 us
  Pallas kernels  33.3 us (97%)
  local copies, waits for them, and re-layouts  0.8 us (2%)
    pallas_call x1, Pallas kernels, shards(): pl.pallas_call(body, name='layers', out_shape=jax.ShapeDtypeStruct((1, ro...  33.3 us
    unnamed x1, local copies, waits for them, and re-layouts  0.8 us

profile of v10, /device:TPU:1, one launch (start us, length us, event | category | flops | bytes accessed | tf_op | source)
XLA Modules:
  0.0 34.1 jit_solution(2207570098432149645)
XLA Ops:
  0.0 33.3 %layers.1 = bf16[1,128,2048]{2,1,0:T(8,128)(2,1)S(1)} custom-call(bf16[128,2048]{1,0:T(8,128)(2,1)} %refs_0_.1, f32[1,2048]{1,0:T(1,128)} %refs_1_.1, bf16[1,2048,3072]{2,1,0:T(8,128)(2,1)} %refs_2_.1, bf16[1,16,2048]{2,1,0:T(8,128)(2,1)} %bitcast.1, f32[1,16]{1,0:T(1,128)} %refs_4_.1, f32[1,16,64,64]{3,2,1,0:T(8,128)} %refs_5_.1, bf16[1,1024,2048]{2,1,0:T(8,128)(2,1)} %refs_6_.1), custom_call_target="tpu_custom_call" | custom-call | tf_op jit(solution)/shard_map/layers/pallas_call | solution.py:491
  33.3 0.8 %copy.9 = bf16[1,128,2048]{2,1,0:T(8,128)(2,1)} copy(bf16[1,128,2048]{2,1,0:T(8,128)(2,1)S(1)} %layers.1) | data formatting | bytes 1048576
